TPU v7x, 128 devices: a whole 4x4x4 slice. The times are simulated.
128 devices in a mesh: row: 8 (over x, y_hi), col: 16 (over y_lo, z, core).
Axes of the slice: x: 4, y: 4 (y_hi: 2, y_lo: 2; y = y_hi * 2 + y_lo), z: 4, core: 2. Of those that a mesh axis runs over, the one named last changes fastest.
Arguments:
- ancestor: float32 [24576, 24576], P('row', 'col'), may hold values from -6 to 6
- panels: float32 [4, 16, 256, 512], P(None, 'col'), may hold values from -0.09375 to 0.09375
- diag_inverse: float32 [4, 512, 512], P(None, 'row'), may hold values from -6 to 6
- fill_strips: int32 [4, 16], replicated, may hold values from 0 to 95, as said below
Outputs:
- upper_strips: float32 [4, 16, 256, 512], P(None, 'col')
- diagonal_blocks: float32 [4, 512, 512], P(None, 'row')
Inputs may be any that keep to these rules, and one draw needn't show every extreme that they name: `fill_strips`: each row lists 16 different strips in no particular order; of the strips s with the same s // 6 a row lists at most 2, and exactly 2 for some value; of the strips with the same s // 12 it lists at most 4, and exactly that many for some value.
All inputs are finite; a program needn't handle non-finite values.
Results may differ from a plain program's by a relative error of at most 0.0001.
Values sent between devices are 32-bit elements; how exact they have to be, the bound alone decides.
No kernel may reach another device: no remote copies, remote signals or barrier semaphores. Data moves between devices by JAX's collectives and lax.ppermute only.
A program may use at most 192 MiB of HBM per device.

v0:
```python
import functools

import jax
import jax.numpy as jnp
from jax import lax
from jax.experimental import pallas as pl
from jax.experimental.pallas import tpu as pltpu
from jax.sharding import Mesh
from jax.sharding import PartitionSpec as P


AXES = ("x", "h", "l", "z", "c")
SIZES = (4, 2, 2, 4, 2)
ROW, COL, PLANE = ("x", "h"), ("l", "z", "c"), ("l", "z")
SHEET = ("h", *PLANE)
S = 256
W = 512
K = 4
F = 16
HALF = W // 2
FRONT = S // 8
PIECE = S // 16
STEPS = (0, 3, 1, 2)
LIMIT = 60 * 1024 * 1024


def col_of(strip):
    return (strip * 43) >> 8


def row_of(strip):
    return col_of(strip) >> 1


def split(value):
    high = value.astype(jnp.bfloat16)
    low = (value - high.astype(jnp.float32)).astype(jnp.bfloat16)
    return high, low


def dot3(left, right, dims):
    (lh, ll), (rh, rl) = left, right
    one = functools.partial(
        lax.dot_general, dimension_numbers=(dims, ((), ())), preferred_element_type=jnp.float32
    )
    return one(lh, rh) + (one(lh, rl) + one(ll, rh))


def pack_kernel(info, fs, panel, out):
    for ch in range(2):
        out[:, ch] = panel[0, 0, :, ch * HALF : (ch + 1) * HALF].reshape(8, FRONT, HALF)


def count_if(fs, k, test):
    total = jnp.int32(0)
    for p in range(F):
        total = total + test(fs[k, p]).astype(jnp.int32)
    return total


def gather_kernel(info, fs, ancestor, after, first, rest, tiles, rows, cols, sems, out_sems):
    r = info[0] * 2 + info[1]
    col = info[2] * 2 + info[3]
    moves = []
    for n, step in enumerate(STEPS):
        k = (info[0] + step) & 3
        nr = jnp.int32(0)
        nc = jnp.int32(0)
        for i in range(8):
            rows[n * 8 + i] = r * 12
        for i in range(4):
            cols[n * 4 + i] = col * 6
        for p in range(F):
            strip = fs[k, p]
            rows[n * 8 + jnp.minimum(nr, 7)] = strip
            cols[n * 4 + jnp.minimum(nc, 3)] = strip
            nr = nr + (row_of(strip) == r).astype(jnp.int32)
            nc = nc + (col_of(strip) == col).astype(jnp.int32)
        for i in range(4):
            low = pl.multiple_of(jnp.clip(rows[n * 8 + i] - r * 12, 0, 11) * S, S)
            for j in range(2):
                left = pl.multiple_of(jnp.clip(cols[n * 4 + j] - col * 6, 0, 5) * S, S)
                valid = jnp.logical_and(i < nr, j < nc)
                source = ancestor.at[pl.ds(low, S), pl.ds(left, S)]
                target = first.at[0, j, i] if n == 0 else rest.at[n - 1, j, i]
                inward = pltpu.make_async_copy(source, tiles.at[n, i, j], sems.at[n, i, j])
                outward = pltpu.make_async_copy(tiles.at[n, i, j], target, out_sems.at[n, i, j])
                pl.when(valid)(inward.start)
                moves.append((valid, inward, outward))
    for valid, inward, outward in moves:

        @pl.when(valid)
        def _():
            inward.wait()
            outward.start()

    for valid, inward, outward in moves:
        pl.when(valid)(outward.wait)


def route_kernel(info, fs, pieces, out, table, count):
    x = info[0]
    for i in range(2 * F):
        table[i] = 0
    for i in range(F):
        count[i] = 0
    for p in range(F):
        col = col_of(fs[x, p])
        n = count[col]
        table[col * 2 + jnp.minimum(n, 1)] = p
        count[col] = n + 1
    for i in range(2 * F):
        out[i] = pieces[table[i]]


def product_kernel(steps, base, info, fs, mine, theirs, *refs):
    out, tiles, sems = refs[-3:]
    refs = list(refs[:-3])
    x, c = info[0], info[3]
    r = x * 2 + info[1]
    col = info[2] * 2 + c
    jobs = []
    for n, step in enumerate(steps):
        k = (x + step) & 3
        nr = jnp.minimum(count_if(fs, k, lambda strip: row_of(strip) == r), 4)
        for side, source in enumerate((mine, theirs)):
            nc = count_if(fs, k, lambda strip: col_of(strip) == (col ^ side))
            for j in range(2):
                spot = (n, side, j)
                loop = jnp.where(j < nc, nr, 0)

                def copy(i, n=base + n, j=j, source=source, spot=spot):
                    return pltpu.make_async_copy(
                        source.at[n, j, i], tiles.at[(*spot, i)], sems.at[(*spot, i)]
                    )

                def start(i, carry, copy=copy):
                    copy(i).start()
                    return carry

                lax.fori_loop(0, loop, start, 0)
                jobs.append((n, (c ^ side) * 2 + j, spot, loop, copy))
    out[...] = jnp.zeros_like(out)
    panels = []
    for step in steps:
        panels.append([refs.pop(0) for _ in range(2 if step == 2 else 1)])
    for n, slot, spot, loop, copy in jobs:

        @pl.when(loop > 0)
        def _():
            right = split(
                jnp.concatenate([ref[:, slot] for ref in panels[n]], axis=0).reshape(S, HALF)
            )

            def body(i, carry):
                copy(i).wait()
                value = dot3(split(tiles[(*spot, i)]), right, ((1,), (0,)))
                out[:, n, i] += value.reshape(16, PIECE, HALF)
                return carry

            lax.fori_loop(0, loop, body, 0)


def homes_kernel(info, fs, *refs):
    pieces, out, table, count = refs[:4], refs[4], refs[5], refs[6]
    x = info[0]
    for i in range(8):
        count[i] = 0
    for p in range(F):
        r = row_of(fs[x, p])
        n = count[r]
        table[r * 4 + jnp.minimum(n, 3)] = p
        count[r] = n + 1
    for dx in range(4):
        for h in range(2):
            r = ((x + dx) & 3) * 2 + h
            for i in range(4):

                @pl.when(i < count[r])
                def _():
                    p = table[r * 4 + i]
                    piece = pieces[dx][h, i]
                    out[p] = piece
                    out[F + p] = piece


def strip_kernel(info, fs, pieces, panel, strip, upper, keep, send, tmp):
    h, c = info[1], info[3]
    parts = [pieces[:, ch].reshape(S, HALF) for ch in range(2)]
    value = jnp.concatenate(parts, axis=1)
    strip[...] = -value
    upper[0, 0] = -value
    tmp[...] = dot3(split(panel[0, 0]), split(value), ((0,), (0,)))
    for xx in range(4):
        low = pl.multiple_of((xx * 2 + h) * 64, 64)
        for out, ch in ((keep, c), (send, 1 - c)):
            lanes = pl.multiple_of(ch * HALF, HALF)
            out[:, xx] = tmp[pl.ds(low, 64), pl.ds(lanes, HALF)].reshape(8, 8, HALF)


VMEM = pl.BlockSpec(memory_space=pltpu.VMEM)
ANY = pl.BlockSpec(memory_space=pl.ANY)


def call(kernel, info, fs, args, out_shapes, in_specs=None, out_specs=None, scratch=(), flops=0):
    single = not isinstance(out_shapes, list)
    shapes = [out_shapes] if single else out_shapes
    out_shape = [jax.ShapeDtypeStruct(s, jnp.float32) for s in shapes]
    moved = 4 * sum(functools.reduce(lambda a, b: a * b, s) for s in shapes)
    return pl.pallas_call(
        kernel,
        out_shape=out_shape[0] if single else out_shape,
        grid_spec=pltpu.PrefetchScalarGridSpec(
            num_scalar_prefetch=2,
            grid=(1,),
            in_specs=in_specs or [VMEM] * len(args),
            out_specs=out_specs or (VMEM if single else [VMEM] * len(shapes)),
            scratch_shapes=list(scratch),
        ),
        compiler_params=pltpu.CompilerParams(vmem_limit_bytes=LIMIT),
        cost_estimate=pl.CostEstimate(flops=flops, bytes_accessed=2 * moved, transcendentals=0),
    )(info, fs, *args)


def hop(value, axis, shift):
    size = SIZES[AXES.index(axis)]
    return lax.ppermute(value, axis, [(i, (i + shift) % size) for i in range(size)])


def exchange(value, axes):
    return lax.all_to_all(value, axes, 0, 0, tiled=True)


def gather_x(value):
    half = value.shape[0] // 2
    before = hop(value, "x", 1)
    after = hop(value, "x", -1)
    top = hop(before[:half], "x", 1)
    bottom = hop(after[half:], "x", -1)
    return before, after, top, bottom


def local(ancestor, panels, diag_inverse, fs):
    x, h, c = lax.axis_index("x"), lax.axis_index("h"), lax.axis_index("c")
    info = jnp.stack([x, h, lax.axis_index(PLANE), c]).astype(jnp.int32)
    own_panel = pl.BlockSpec((1, 1, S, W), lambda i, info, fs: (info[0], 0, 0, 0))

    packed = call(pack_kernel, info, fs, [panels], (8, 2, FRONT, HALF), in_specs=[own_panel])
    pieces = exchange(packed.reshape(F, FRONT, HALF), COL)
    routed = call(
        route_kernel, info, fs, [pieces], (2 * F, FRONT, HALF),
        scratch=[pltpu.SMEM((2 * F,), jnp.int32), pltpu.SMEM((F,), jnp.int32)],
    )
    panel = exchange(routed.reshape(8, 4, FRONT, HALF), PLANE)
    first_tiles, rest_tiles = call(
        gather_kernel, info, fs, [ancestor, packed], [(1, 2, 4, S, S), (3, 2, 4, S, S)],
        in_specs=[ANY, ANY], out_specs=[ANY, ANY],
        scratch=[pltpu.VMEM((K, 4, 2, S, S), jnp.float32),
                 pltpu.SMEM((K * 8,), jnp.int32), pltpu.SMEM((K * 4,), jnp.int32),
                 pltpu.SemaphoreType.DMA((K, 4, 2)), pltpu.SemaphoreType.DMA((K, 4, 2))],
    )
    first_pair = [first_tiles, hop(first_tiles, "c", 1)]
    rest_pair = [rest_tiles, hop(rest_tiles, "c", 1)]
    before, after, top, bottom = gather_x(panel)

    def product(steps, base, pair, blocks, behind=()):
        n = len(steps)
        return call(
            functools.partial(product_kernel, steps, base), info, fs,
            [*pair, *blocks, *behind], (16, n, 4, PIECE, HALF),
            in_specs=[ANY] * 2 + [VMEM] * len(blocks) + [ANY] * len(behind),
            scratch=[pltpu.VMEM((n, 2, 2, 4, S, S), jnp.float32),
                     pltpu.SemaphoreType.DMA((n, 2, 2, 4))],
            flops=n * 10**9,
        )

    def total(value):
        value = exchange(value, SHEET)
        value = value.reshape(2, 8, *value.shape[1:]).sum(1)
        return [value[:, n] for n in range(value.shape[1])]

    own_product = product((0,), 0, first_pair, [panel])
    (own,) = total(own_product)
    near_product = product((3, 1), 0, rest_pair, [before, after], [own])
    near = total(near_product)
    far_product = product((2,), 2, rest_pair, [top, bottom], [near_product])
    near, far_product = lax.optimization_barrier((near, far_product))
    (far,) = total(far_product)
    sources = [own, hop(near[0], "x", -1), hop(far, "x", 2), hop(near[1], "x", 1)]
    homes = call(
        homes_kernel, info, fs, sources, (2 * F, PIECE, HALF),
        scratch=[pltpu.SMEM((32,), jnp.int32), pltpu.SMEM((8,), jnp.int32)],
    )
    placed = exchange(homes, ("h", *COL)).reshape(16, 2, PIECE, HALF)
    strip, upper, part, part_send = call(
        strip_kernel, info, fs, [placed, panels],
        [(S, W), (K, 1, S, W), (8, 4, 8, HALF), (8, 4, 8, HALF)], in_specs=[VMEM, own_panel],
        out_specs=[VMEM, own_panel, VMEM, VMEM],
        scratch=[pltpu.VMEM((W, W), jnp.float32)],
    )
    before, after, top, bottom = gather_x(strip)
    part = exchange(part + hop(part_send, "c", 1), PLANE).sum(0)
    part = exchange(part, ("x",))
    part = exchange(jnp.broadcast_to(part[None], (8, *part.shape)), PLANE)
    for value, step, low in ((before, 3, 0), (after, 1, 0), (top, 2, 0), (bottom, 2, S // 2)):
        k = (x + step) & 3
        upper = lax.dynamic_update_slice(upper, value[None, None], (k, 0, low, 0))
    part = part.transpose(1, 0, 2, 3).reshape(K, 64, HALF)
    theirs = hop(part, "c", 1)
    diagonal = diag_inverse + jnp.where(
        c == 0,
        jnp.concatenate([part, theirs], axis=2),
        jnp.concatenate([theirs, part], axis=2),
    )
    return upper, diagonal


def solution(mesh):
    return jax.shard_map(
        local,
        mesh=Mesh(mesh.devices.reshape(SIZES), AXES),
        in_specs=(P(ROW, COL), P(None, COL, None, None), P(None, ROW, None), P()),
        out_specs=(P(None, COL, None, None), P(None, ROW, None)),
        check_vma=False,
    )
```

profile of v0, /device:TPU:1, one launch (start us, length us, event | category | flops | bytes accessed | tf_op | source)
XLA Modules:
  0.0 216.6 jit_solution(8477949231602225308)
XLA Ops:
  1.3 2.6 %shard_map.59.after = f32[8,2,32,256]{3,2,1,0:T(8,128)} custom-call(s32[4]{0:T(128)} %pad_add_fusion.info, s32[4,16]{1,0:T(4,128)} %fs.15, f32[4,1,256,512]{3,2,1,0:T(8,128)} %panel.3), custom_call_target="tpu_custom_call" | custom-call | bytes 1048576 | tf_op jit(solution)/shard_map/pallas_call | solution.py:210
  3.8 4.6 %shard_map.60 = (f32[1,2,4,256,256]{4,3,2,1,0:T(8,128)}, f32[3,2,4,256,256]{4,3,2,1,0:T(8,128)}) custom-call(s32[4]{0:T(128)} %pad_add_fusion.info, s32[4,16]{1,0:T(4,128)} %fs.15, f32[3072,1536]{1,0:T(8,128)} %ancestor.1, f32[8,2,32,256]{3,2,1,0:T(8,128)} %shard_map.59.after), custom_call_target="tpu_custom_call" | custom-call | bytes 16777216 | tf_op jit(solution)/shard_map/pallas_call | solution.py:210
  8.4 1.2 collective-permute-start.1
  9.7 16.2 %all_to_all.45.pieces = f32[16,32,256]{2,1,0:T(8,128)} all-to-all(f32[16,32,256]{2,1,0:T(8,128)S(1)} %bitcast.36), channel_id=1, replica_groups=mesh['x'=4,'h'=2,'l'=2,'z'=4,'c'=2] {'l','z','c'}, dimensions={0} | all-to-all | bytes 1048576 | tf_op jit(solution)/shard_map/all_to_all | solution.py:231
  25.9 2.8 %shard_map.61 = f32[32,32,256]{2,1,0:T(8,128)} custom-call(s32[4]{0:T(128)} %pad_add_fusion.info, s32[4,16]{1,0:T(4,128)} %fs.15, f32[16,32,256]{2,1,0:T(8,128)} %all_to_all.45.pieces), custom_call_target="tpu_custom_call" | custom-call | bytes 2097152 | tf_op jit(solution)/shard_map/pallas_call | solution.py:210
  28.8 18.1 %all_to_all.46.refs_0_ = f32[8,4,32,256]{3,2,1,0:T(8,128)} all-to-all(f32[8,4,32,256]{3,2,1,0:T(8,128)} %bitcast.39), channel_id=1, replica_groups=mesh['x'=4,'h'=2,'l'=2,'z'=4,'c'=2] {'l','z'}, dimensions={0} | all-to-all | bytes 2097152 | tf_op jit(solution)/shard_map/all_to_all | solution.py:231
  46.9 1.3 copy-done.4
  48.2 4.3 %shard_map.62 = f32[16,1,4,16,256]{4,3,2,1,0:T(8,128)} custom-call(s32[4]{0:T(128)} %pad_add_fusion.info, s32[4,16]{1,0:T(4,128)} %fs.15, f32[1,2,4,256,256]{4,3,2,1,0:T(8,128)} %get-tuple-element.11.mine, f32[1,2,4,256,256]{4,3,2,1,0:T(8,128)} %copy-done.4, f32[8,4,32,256]{3,2,1,0:T(8,128)} %all_to_all.46.refs_0_), custom_call_target="tpu_custom_call" | custom-call | flops 1000000000 | bytes 2097152 | tf_op jit(solution)/shard_map/pallas_call | solution.py:210
  52.4 5.4 %all-to-all-start.2 = ((f32[16,1,4,16,256]{4,3,2,1,0:T(8,128)}), f32[16,1,4,16,256]{4,3,2,1,0:T(8,128)S(1)}, u32[]{:S(2)}, u32[]{:S(2)}) async-start(f32[16,1,4,16,256]{4,3,2,1,0:T(8,128)} %shard_map.62), calls=%async_computation.2 | async-start | bytes 2097152 | tf_op jit(solution)/shard_map/all_to_all | solution.py:231
  57.9 2.8 %collective-permute-start.2 = (f32[8,4,32,256]{3,2,1,0:T(8,128)S(1)}, f32[8,4,32,256]{3,2,1,0:T(8,128)}, u32[]{:S(2)}, u32[]{:S(2)}) collective-permute-start(f32[8,4,32,256]{3,2,1,0:T(8,128)S(1)} %copy-done.1), channel_id=1, source_target_pairs={{0,32},{32,64},{64,96},{96,0},{1,33},{33,65},{65,97},{97,1},{2,34}... | collective-permute-start | bytes 3145736 | tf_op jit(solution)/shard_map/ppermute | solution.py:227
  60.8 1.1 collective-permute-start.3
  61.9 10.7 %all-to-all-done.2 = f32[16,1,4,16,256]{4,3,2,1,0:T(8,128)S(1)} async-done(((f32[16,1,4,16,256]{4,3,2,1,0:T(8,128)}), f32[16,1,4,16,256]{4,3,2,1,0:T(8,128)S(1)}, u32[]{:S(2)}, u32[]{:S(2)}) %all-to-all-start.2) | async-done | bytes 1048608 | tf_op jit(solution)/shard_map/all_to_all | solution.py:231
  73.2 9.2 %collective-permute-done.2.refs_0_ = f32[8,4,32,256]{3,2,1,0:T(8,128)} collective-permute-done((f32[8,4,32,256]{3,2,1,0:T(8,128)S(1)}, f32[8,4,32,256]{3,2,1,0:T(8,128)}, u32[]{:S(2)}, u32[]{:S(2)}) %collective-permute-start.2) | collective-permute-done | bytes 1048608 | tf_op jit(solution)/shard_map/ppermute | solution.py:227
  83.1 1.0 copy-done.2
  84.1 10.5 %shard_map.63.refs_2_ = f32[16,2,4,16,256]{4,3,2,1,0:T(8,128)} custom-call(s32[4]{0:T(128)} %pad_add_fusion.info, s32[4,16]{1,0:T(4,128)} %fs.15, f32[3,2,4,256,256]{4,3,2,1,0:T(8,128)} %get-tuple-element.12.mine, f32[3,2,4,256,256]{4,3,2,1,0:T(8,128)} %collective-permute-done.1.theirs, f32[8,4,32,256]{3,2,1,0:T(8,128)} %collective-permute-done.2.refs_0_, ...), custom_call_target="tpu_custom_call" | custom-call | flops 2000000000 | bytes 4194304 | tf_op jit(solution)/shard_map/pallas_call | solution.py:210
  94.6 3.9 %all-to-all-start.3 = ((f32[16,2,4,16,256]{4,3,2,1,0:T(8,128)}), f32[16,2,4,16,256]{4,3,2,1,0:T(8,128)S(1)}, u32[]{:S(2)}, u32[]{:S(2)}) async-start(f32[16,2,4,16,256]{4,3,2,1,0:T(8,128)} %shard_map.63.refs_2_), calls=%async_computation.3 | async-start | bytes 4194304 | tf_op jit(solution)/shard_map/all_to_all | solution.py:231
  98.5 1.1 slice.26
  99.6 1.8 collective-permute-start.4
  101.5 1.0 collective-permute-start.5
  102.4 8.3 %collective-permute-done.4.refs_0_ = f32[4,4,32,256]{3,2,1,0:T(8,128)S(1)} collective-permute-done((f32[4,4,32,256]{3,2,1,0:T(8,128)S(1)}, f32[4,4,32,256]{3,2,1,0:T(8,128)S(1)}, u32[]{:S(2)}, u32[]{:S(2)}) %collective-permute-start.4) | collective-permute-done | bytes 524320 | tf_op jit(solution)/shard_map/ppermute | solution.py:227
  110.8 0.7 copy-done.6
  111.5 0.8 copy-done.7
  112.3 5.2 %shard_map.64 = f32[16,1,4,16,256]{4,3,2,1,0:T(8,128)} custom-call(s32[4]{0:T(128)} %pad_add_fusion.info, s32[4,16]{1,0:T(4,128)} %fs.15, f32[3,2,4,256,256]{4,3,2,1,0:T(8,128)} %get-tuple-element.12.mine, f32[3,2,4,256,256]{4,3,2,1,0:T(8,128)} %collective-permute-done.1.theirs, f32[4,4,32,256]{3,2,1,0:T(8,128)} %copy-done.6, f32[4,4,32,256]{3,2,1,0:T(8,128)} %copy-done.7, ...), custom_call_target="tpu_custom_call" | custom-call | flops 1000000000 | bytes 2097152 | tf_op jit(solution)/shard_map/pallas_call | solution.py:210
  117.5 6.1 %all-to-all-done.3 = f32[16,2,4,16,256]{4,3,2,1,0:T(8,128)S(1)} async-done(((f32[16,2,4,16,256]{4,3,2,1,0:T(8,128)}), f32[16,2,4,16,256]{4,3,2,1,0:T(8,128)S(1)}, u32[]{:S(2)}, u32[]{:S(2)}) %all-to-all-start.3) | async-done | bytes 2097184 | tf_op jit(solution)/shard_map/all_to_all | solution.py:231
  123.9 5.8 %all-to-all-start.4 = ((f32[16,1,4,16,256]{4,3,2,1,0:T(8,128)}), f32[16,1,4,16,256]{4,3,2,1,0:T(8,128)S(1)}, u32[]{:S(2)}, u32[]{:S(2)}) async-start(f32[16,1,4,16,256]{4,3,2,1,0:T(8,128)} %shard_map.64), calls=%async_computation.4 | async-start | bytes 2097152 | tf_op jit(solution)/shard_map/all_to_all | solution.py:231
  129.7 1.8 collective-permute-start.6
  131.5 10.2 %all-to-all-done.4 = f32[16,1,4,16,256]{4,3,2,1,0:T(8,128)S(1)} async-done(((f32[16,1,4,16,256]{4,3,2,1,0:T(8,128)}), f32[16,1,4,16,256]{4,3,2,1,0:T(8,128)S(1)}, u32[]{:S(2)}, u32[]{:S(2)}) %all-to-all-start.4) | async-done | bytes 1048608 | tf_op jit(solution)/shard_map/all_to_all | solution.py:231
  141.8 0.7 collective-permute-start.7
  142.5 4.8 %collective-permute-done.7.refs_2_ = f32[2,4,16,256]{3,2,1,0:T(8,128)S(1)} collective-permute-done((f32[2,4,16,256]{3,2,1,0:T(8,128)S(1)}, f32[2,4,16,256]{3,2,1,0:T(8,128)S(1)}, u32[]{:S(2)}, u32[]{:S(2)}) %collective-permute-start.7) | collective-permute-done | bytes 131104 | tf_op jit(solution)/shard_map/ppermute | solution.py:227
  148.0 2.8 %shard_map.65 = f32[32,16,256]{2,1,0:T(8,128)} custom-call(s32[4]{0:T(128)} %pad_add_fusion.info, s32[4,16]{1,0:T(4,128)} %fs.15, f32[2,4,16,256]{3,2,1,0:T(8,128)} %bitcast_reduce_fusion.2.refs_2_.refs_0_, f32[2,4,16,256]{3,2,1,0:T(8,128)} %copy-done.8, f32[2,4,16,256]{3,2,1,0:T(8,128)} %copy-done.10, f32[2,4,16,256]{3,2,1,0:T(8,128)} %copy-done.9), custom_call_target="tpu_custom_call" | custom-call | bytes 1048576 | tf_op jit(solution)/shard_map/pallas_call | solution.py:210
  150.8 23.1 %all_to_all.47 = f32[32,16,256]{2,1,0:T(8,128)} all-to-all(f32[32,16,256]{2,1,0:T(8,128)} %shard_map.65), channel_id=1, replica_groups=mesh['x'=4,'h'=2,'l'=2,'z'=4,'c'=2] {'h','l','z','c'}, dimensions={0} | all-to-all | bytes 1048576 | tf_op jit(solution)/shard_map/all_to_all | solution.py:231
  173.9 3.4 %shard_map.66 = (f32[256,512]{1,0:T(8,128)}, f32[4,1,256,512]{3,2,1,0:T(8,128)}, f32[8,4,8,256]{3,2,1,0:T(8,128)}, f32[8,4,8,256]{3,2,1,0:T(8,128)}) custom-call(s32[4]{0:T(128)} %pad_add_fusion.info, s32[4,16]{1,0:T(4,128)} %fs.15, f32[16,2,16,256]{3,2,1,0:T(8,128)} %bitcast.40, f32[4,1,256,512]{3,2,1,0:T(8,128)} %panel.3), custom_call_target="tpu_custom_call" | custom-call | bytes 6291456 | tf_op jit(solution)/shard_map/pallas_call | solution.py:210
  177.3 1.6 collective-permute-start.9
  178.9 1.1 collective-permute-start.10
  180.2 1.5 collective-permute-done.13
  181.7 1.0 add.36
  182.7 8.8 %all_to_all.48 = f32[8,4,8,256]{3,2,1,0:T(8,128)S(1)} all-to-all(f32[8,4,8,256]{3,2,1,0:T(8,128)S(1)} %add.36), channel_id=1, replica_groups=mesh['x'=4,'h'=2,'l'=2,'z'=4,'c'=2] {'l','z'}, dimensions={0} | all-to-all | bytes 524288 | tf_op jit(solution)/shard_map/all_to_all | solution.py:231
  192.1 3.3 %all-to-all-start.7 = ((f32[4,8,256]{2,1,0:T(8,128)}), f32[4,8,256]{2,1,0:T(8,128)S(1)}, u32[]{:S(2)}, u32[]{:S(2)}) async-start(f32[4,8,256]{2,1,0:T(8,128)} %reduce_sum.39), calls=%async_computation.7 | async-start | bytes 65536 | tf_op jit(solution)/shard_map/all_to_all | solution.py:231
  195.4 4.3 %all-to-all-done.7 = f32[4,8,256]{2,1,0:T(8,128)S(1)} async-done(((f32[4,8,256]{2,1,0:T(8,128)}), f32[4,8,256]{2,1,0:T(8,128)S(1)}, u32[]{:S(2)}, u32[]{:S(2)}) %all-to-all-start.7) | async-done | bytes 32800 | tf_op jit(solution)/shard_map/all_to_all | solution.py:231
  200.4 3.4 %all-to-all-start.8 = ((f32[8,4,8,256]{3,2,1,0:T(8,128)}), f32[8,4,8,256]{3,2,1,0:T(8,128)S(1)}, u32[]{:S(2)}, u32[]{:S(2)}) async-start(f32[8,4,8,256]{3,2,1,0:T(8,128)} %broadcast_in_dim.22), calls=%async_computation.8 | async-start | bytes 524288 | tf_op jit(solution)/shard_map/all_to_all | solution.py:231
  204.2 2.5 %collective-permute-start.12 = (f32[128,512]{1,0:T(8,128)S(1)}, f32[128,512]{1,0:T(8,128)S(1)}, u32[]{:S(2)}, u32[]{:S(2)}) collective-permute-start(f32[128,512]{1,0:T(8,128)S(1)} %slice.29), channel_id=1, source_target_pairs={{0,96},{32,0},{64,32},{96,64},{1,97},{33,1},{65,33},{97,65},{2,98}... | collective-permute-start | bytes 786440 | tf_op jit(solution)/shard_map/ppermute | solution.py:227
  206.7 0.8 bitcast_dynamic-update-slice_fusion.1
  207.5 0.8 bitcast_dynamic-update-slice_fusion
  208.4 1.5 all-to-all-done.8
  209.9 4.3 %collective-permute-start.14 = (f32[4,64,256]{2,1,0:T(8,128)S(1)}, f32[4,64,256]{2,1,0:T(8,128)S(1)}, u32[]{:S(2)}, u32[]{:S(2)}) collective-permute-start(f32[4,64,256]{2,1,0:T(8,128)S(1)} %bitcast.41), channel_id=1, source_target_pairs={{0,1},{1,0},{2,3},{3,2},{4,5},{5,4},{6,7},{7,6},{8,9},{9,8},{10,11... | collective-permute-start | bytes 786440 | tf_op jit(solution)/shard_map/ppermute | solution.py:227
  214.2 0.7 bitcast_dynamic-update-slice_fusion.3
  214.9 0.7 bitcast_dynamic-update-slice_fusion.2
  215.7 0.9 fusion
  (44 shorter events, 5.3 us)
Async XLA Ops:
  3.8 5.8 %copy-start = (f32[8,2,32,256]{3,2,1,0:T(8,128)S(1)}, f32[8,2,32,256]{3,2,1,0:T(8,128)}, u32[]{:S(2)}) copy-start(f32[8,2,32,256]{3,2,1,0:T(8,128)} %shard_map.59.after) | copy-start | bytes 1572868
  8.4 74.7 %collective-permute-start.1 = (f32[3,2,4,256,256]{4,3,2,1,0:T(8,128)}, f32[3,2,4,256,256]{4,3,2,1,0:T(8,128)}, u32[]{:S(2)}, u32[]{:S(2)}) collective-permute-start(f32[3,2,4,256,256]{4,3,2,1,0:T(8,128)} %get-tuple-element.12.mine), channel_id=1, source_target_pairs={{0,1},{1,0},{2,3},{3,2},{4,5},{5,4},{6,7},{7,6},{8,9},{9,8},{10,11... | collective-permute-start | bytes 18874376 | tf_op jit(solution)/shard_map/ppermute | solution.py:227
  9.6 37.3 %collective-permute-start = (f32[1,2,4,256,256]{4,3,2,1,0:T(8,128)}, f32[1,2,4,256,256]{4,3,2,1,0:T(8,128)S(1)}, u32[]{:S(2)}, u32[]{:S(2)}) collective-permute-start(f32[1,2,4,256,256]{4,3,2,1,0:T(8,128)} %get-tuple-element.11.mine), channel_id=1, source_target_pairs={{0,1},{1,0},{2,3},{3,2},{4,5},{5,4},{6,7},{7,6},{8,9},{9,8},{10,11... | collective-permute-start | bytes 6291464 | tf_op jit(solution)/shard_map/ppermute | solution.py:227
  46.9 1.3 copy-start.4
  52.4 5.5 %copy-start.1 = (f32[8,4,32,256]{3,2,1,0:T(8,128)S(1)}, f32[8,4,32,256]{3,2,1,0:T(8,128)}, u32[]{:S(2)}) copy-start(f32[8,4,32,256]{3,2,1,0:T(8,128)} %all_to_all.46.refs_0_) | copy-start | bytes 3145732
  52.4 20.1 %all-to-all-start.2 = ((f32[16,1,4,16,256]{4,3,2,1,0:T(8,128)}), f32[16,1,4,16,256]{4,3,2,1,0:T(8,128)S(1)}, u32[]{:S(2)}, u32[]{:S(2)}) async-start(f32[16,1,4,16,256]{4,3,2,1,0:T(8,128)} %shard_map.62), calls=%async_computation.2 | async-start | bytes 2097152 | tf_op jit(solution)/shard_map/all_to_all | solution.py:231
  57.9 24.5 %collective-permute-start.2 = (f32[8,4,32,256]{3,2,1,0:T(8,128)S(1)}, f32[8,4,32,256]{3,2,1,0:T(8,128)}, u32[]{:S(2)}, u32[]{:S(2)}) collective-permute-start(f32[8,4,32,256]{3,2,1,0:T(8,128)S(1)} %copy-done.1), channel_id=1, source_target_pairs={{0,32},{32,64},{64,96},{96,0},{1,33},{33,65},{65,97},{97,1},{2,34}... | collective-permute-start | bytes 3145736 | tf_op jit(solution)/shard_map/ppermute | solution.py:227
  60.8 22.4 %collective-permute-start.3 = (f32[8,4,32,256]{3,2,1,0:T(8,128)S(1)}, f32[8,4,32,256]{3,2,1,0:T(8,128)S(1)}, u32[]{:S(2)}, u32[]{:S(2)}) collective-permute-start(f32[8,4,32,256]{3,2,1,0:T(8,128)S(1)} %copy-done.1), channel_id=1, source_target_pairs={{0,96},{32,0},{64,32},{96,64},{1,97},{33,1},{65,33},{97,65},{2,98}... | collective-permute-start | bytes 3145736 | tf_op jit(solution)/shard_map/ppermute | solution.py:227
  83.1 1.0 copy-start.2
  94.6 6.8 %copy-start.3 = (f32[8,4,32,256]{3,2,1,0:T(8,128)S(1)}, f32[8,4,32,256]{3,2,1,0:T(8,128)}, u32[]{:S(2)}) copy-start(f32[8,4,32,256]{3,2,1,0:T(8,128)} %copy-done.2) | copy-start | bytes 3145732
  94.6 29.0 %all-to-all-start.3 = ((f32[16,2,4,16,256]{4,3,2,1,0:T(8,128)}), f32[16,2,4,16,256]{4,3,2,1,0:T(8,128)S(1)}, u32[]{:S(2)}, u32[]{:S(2)}) async-start(f32[16,2,4,16,256]{4,3,2,1,0:T(8,128)} %shard_map.63.refs_2_), calls=%async_computation.3 | async-start | bytes 4194304 | tf_op jit(solution)/shard_map/all_to_all | solution.py:231
  99.6 11.2 %collective-permute-start.4 = (f32[4,4,32,256]{3,2,1,0:T(8,128)S(1)}, f32[4,4,32,256]{3,2,1,0:T(8,128)S(1)}, u32[]{:S(2)}, u32[]{:S(2)}) collective-permute-start(f32[4,4,32,256]{3,2,1,0:T(8,128)S(1)} %slice.26), channel_id=1, source_target_pairs={{0,32},{32,64},{64,96},{96,0},{1,33},{33,65},{65,97},{97,1},{2,34}... | collective-permute-start | bytes 1572872 | tf_op jit(solution)/shard_map/ppermute | solution.py:227
  101.5 9.3 %collective-permute-start.5 = (f32[4,4,32,256]{3,2,1,0:T(8,128)S(1)}, f32[4,4,32,256]{3,2,1,0:T(8,128)S(1)}, u32[]{:S(2)}, u32[]{:S(2)}) collective-permute-start(f32[4,4,32,256]{3,2,1,0:T(8,128)S(1)} %slice.27), channel_id=1, source_target_pairs={{0,96},{32,0},{64,32},{96,64},{1,97},{33,1},{65,33},{97,65},{2,98}... | collective-permute-start | bytes 1572872 | tf_op jit(solution)/shard_map/ppermute | solution.py:227
  110.7 0.8 copy-start.6
  111.5 0.8 copy-start.7
  123.9 17.8 %all-to-all-start.4 = ((f32[16,1,4,16,256]{4,3,2,1,0:T(8,128)}), f32[16,1,4,16,256]{4,3,2,1,0:T(8,128)S(1)}, u32[]{:S(2)}, u32[]{:S(2)}) async-start(f32[16,1,4,16,256]{4,3,2,1,0:T(8,128)} %shard_map.64), calls=%async_computation.4 | async-start | bytes 2097152 | tf_op jit(solution)/shard_map/all_to_all | solution.py:231
  129.7 12.8 %collective-permute-start.6 = (f32[2,4,16,256]{3,2,1,0:T(8,128)S(1)}, f32[2,4,16,256]{3,2,1,0:T(8,128)S(1)}, u32[]{:S(2)}, u32[]{:S(2)}) collective-permute-start(f32[2,4,16,256]{3,2,1,0:T(8,128)S(1)} %get-tuple-element.13), channel_id=1, source_target_pairs={{0,96},{32,0},{64,32},{96,64},{1,97},{33,1},{65,33},{97,65},{2,98}... | collective-permute-start | bytes 393224 | tf_op jit(solution)/shard_map/ppermute | solution.py:227
  131.5 11.1 %collective-permute-start.8 = (f32[2,4,16,256]{3,2,1,0:T(8,128)S(1)}, f32[2,4,16,256]{3,2,1,0:T(8,128)S(1)}, u32[]{:S(2)}, u32[]{:S(2)}) collective-permute-start(f32[2,4,16,256]{3,2,1,0:T(8,128)S(1)} %get-tuple-element.15), channel_id=1, source_target_pairs={{0,32},{32,64},{64,96},{96,0},{1,33},{33,65},{65,97},{97,1},{2,34}... | collective-permute-start | bytes 393224 | tf_op jit(solution)/shard_map/ppermute | solution.py:227
  141.8 5.6 %collective-permute-start.7 = (f32[2,4,16,256]{3,2,1,0:T(8,128)S(1)}, f32[2,4,16,256]{3,2,1,0:T(8,128)S(1)}, u32[]{:S(2)}, u32[]{:S(2)}) collective-permute-start(f32[2,4,16,256]{3,2,1,0:T(8,128)S(1)} %bitcast_reduce_fusion.1), channel_id=1, source_target_pairs={{0,64},{32,96},{64,0},{96,32},{1,65},{33,97},{65,1},{97,33},{2,66}... | collective-permute-start | bytes 393224 | tf_op jit(solution)/shard_map/ppermute | solution.py:227
  142.5 4.8 %copy-start.8 = (f32[2,4,16,256]{3,2,1,0:T(8,128)}, f32[2,4,16,256]{3,2,1,0:T(8,128)S(1)}, u32[]{:S(2)}) copy-start(f32[2,4,16,256]{3,2,1,0:T(8,128)S(1)} %collective-permute-done.6.refs_1_) | copy-start | bytes 393220
  142.5 4.8 %copy-start.9 = (f32[2,4,16,256]{3,2,1,0:T(8,128)}, f32[2,4,16,256]{3,2,1,0:T(8,128)S(1)}, u32[]{:S(2)}) copy-start(f32[2,4,16,256]{3,2,1,0:T(8,128)S(1)} %collective-permute-done.8.refs_3_) | copy-start | bytes 393220
  147.4 0.6 copy-start.10
  177.3 26.5 %collective-permute-start.9 = (f32[256,512]{1,0:T(8,128)}, f32[256,512]{1,0:T(8,128)S(1)}, u32[]{:S(2)}, u32[]{:S(2)}) collective-permute-start(f32[256,512]{1,0:T(8,128)} %get-tuple-element.17), channel_id=1, source_target_pairs={{0,32},{32,64},{64,96},{96,0},{1,33},{33,65},{65,97},{97,1},{2,34}... | collective-permute-start | bytes 1572872 | tf_op jit(solution)/shard_map/ppermute | solution.py:227
  178.9 25.3 %collective-permute-start.10 = (f32[256,512]{1,0:T(8,128)}, f32[256,512]{1,0:T(8,128)S(1)}, u32[]{:S(2)}, u32[]{:S(2)}) collective-permute-start(f32[256,512]{1,0:T(8,128)} %get-tuple-element.17), channel_id=1, source_target_pairs={{0,96},{32,0},{64,32},{96,64},{1,97},{33,1},{65,33},{97,65},{2,98}... | collective-permute-start | bytes 1572872 | tf_op jit(solution)/shard_map/ppermute | solution.py:227
  180.0 1.7 collective-permute-start.13
  192.1 7.5 %all-to-all-start.7 = ((f32[4,8,256]{2,1,0:T(8,128)}), f32[4,8,256]{2,1,0:T(8,128)S(1)}, u32[]{:S(2)}, u32[]{:S(2)}) async-start(f32[4,8,256]{2,1,0:T(8,128)} %reduce_sum.39), calls=%async_computation.7 | async-start | bytes 65536 | tf_op jit(solution)/shard_map/all_to_all | solution.py:231
  200.4 9.5 %all-to-all-start.8 = ((f32[8,4,8,256]{3,2,1,0:T(8,128)}), f32[8,4,8,256]{3,2,1,0:T(8,128)S(1)}, u32[]{:S(2)}, u32[]{:S(2)}) async-start(f32[8,4,8,256]{3,2,1,0:T(8,128)} %broadcast_in_dim.22), calls=%async_computation.8 | async-start | bytes 524288 | tf_op jit(solution)/shard_map/all_to_all | solution.py:231
  203.8 11.8 %copy-start.5 = (f32[4,64,512]{2,1,0:T(8,128)S(1)}, f32[4,64,512]{2,1,0:T(8,128)}, u32[]{:S(2)}) copy-start(f32[4,64,512]{2,1,0:T(8,128)} %param.6) | copy-start | bytes 1572868
  203.9 10.3 %collective-permute-start.11 = (f32[128,512]{1,0:T(8,128)S(1)}, f32[128,512]{1,0:T(8,128)S(1)}, u32[]{:S(2)}, u32[]{:S(2)}) collective-permute-start(f32[128,512]{1,0:T(8,128)S(1)} %slice.28), channel_id=1, source_target_pairs={{0,32},{32,64},{64,96},{96,0},{1,33},{33,65},{65,97},{97,1},{2,34}... | collective-permute-start | bytes 786440 | tf_op jit(solution)/shard_map/ppermute | solution.py:227
  204.2 10.7 %collective-permute-start.12 = (f32[128,512]{1,0:T(8,128)S(1)}, f32[128,512]{1,0:T(8,128)S(1)}, u32[]{:S(2)}, u32[]{:S(2)}) collective-permute-start(f32[128,512]{1,0:T(8,128)S(1)} %slice.29), channel_id=1, source_target_pairs={{0,96},{32,0},{64,32},{96,64},{1,97},{33,1},{65,33},{97,65},{2,98}... | collective-permute-start | bytes 786440 | tf_op jit(solution)/shard_map/ppermute | solution.py:227
  209.9 5.8 %collective-permute-start.14 = (f32[4,64,256]{2,1,0:T(8,128)S(1)}, f32[4,64,256]{2,1,0:T(8,128)S(1)}, u32[]{:S(2)}, u32[]{:S(2)}) collective-permute-start(f32[4,64,256]{2,1,0:T(8,128)S(1)} %bitcast.41), channel_id=1, source_target_pairs={{0,1},{1,0},{2,3},{3,2},{4,5},{5,4},{6,7},{7,6},{8,9},{9,8},{10,11... | collective-permute-start | bytes 786440 | tf_op jit(solution)/shard_map/ppermute | solution.py:227
where the time goes:
time: 218 us; the launch traced here: 217 us
  blocking collectives  66.2 us (30%)
  waiting for transfers between devices  57.3 us (26%)
  starting transfers between devices  42.4 us (19%)
  Pallas kernels  36.1 us (17%)
  local copies, waits for them, and re-layouts  9.47 us (4%)
  other arithmetic  4.15 us (2%)
    all_to_all x4, blocking collectives, exchange(): return lax.all_to_all(value, axes, 0, 0, tiled=True)  66.2 us
    pallas_call x8, Pallas kernels, call(): pl.pallas_call(kernel, out_shape=out_shape[0] if single else out_shape, g...  36.1 us
    all_to_all x5, waiting for transfers between devices, exchange(): return lax.all_to_all(value, axes, 0, 0, tiled=True)  32.8 us
    ppermute x15, waiting for transfers between devices, hop(): lax.ppermute(value, axis, [(i, (i + shift) % size) for i in range(size)])  24.5 us
    all_to_all x5, starting transfers between devices, exchange(): return lax.all_to_all(value, axes, 0, 0, tiled=True)  21.8 us
    ppermute x15, starting transfers between devices, hop(): lax.ppermute(value, axis, [(i, (i + shift) % size) for i in range(size)])  20.7 us
    unnamed x22, local copies, waits for them, and re-layouts  4.47 us
  transfers between devices with their start and end apart: 20, of which 11 were waited for; matrix products, arithmetic and copies ran while one was open for 3% of the time, Pallas kernels for 6%

commit v1 on v0

--- a/solution.py
+++ b/solution.py
@@ -21,7 +21,6 @@
 FRONT = S // 8
 PIECE = S // 16
 STEPS = (0, 3, 1, 2)
-LIMIT = 60 * 1024 * 1024
 
 
 def col_of(strip):
@@ -46,9 +45,12 @@
     return one(lh, rh) + (one(lh, rl) + one(ll, rh))
 
 
-def pack_kernel(info, fs, panel, out):
+def pack_kernel(fs, panels, out, panel, sem):
+    copy = pltpu.make_async_copy(panels.at[lax.axis_index("x"), 0], panel, sem)
+    copy.start()
+    copy.wait()
     for ch in range(2):
-        out[:, ch] = panel[0, 0, :, ch * HALF : (ch + 1) * HALF].reshape(8, FRONT, HALF)
+        out[:, ch] = panel[:, ch * HALF : (ch + 1) * HALF].reshape(8, FRONT, HALF)
 
 
 def count_if(fs, k, test):
@@ -58,12 +60,12 @@
     return total
 
 
-def gather_kernel(info, fs, ancestor, after, first, rest, tiles, rows, cols, sems, out_sems):
-    r = info[0] * 2 + info[1]
-    col = info[2] * 2 + info[3]
+def gather_kernel(fs, ancestor, after, first, rest, tiles, rows, cols, sems, out_sems):
+    r = lax.axis_index("x") * 2 + lax.axis_index("h")
+    col = lax.axis_index(PLANE) * 2 + lax.axis_index("c")
     moves = []
     for n, step in enumerate(STEPS):
-        k = (info[0] + step) & 3
+        k = (lax.axis_index("x") + step) & 3
         nr = jnp.int32(0)
         nc = jnp.int32(0)
         for i in range(8):
@@ -98,8 +100,8 @@
         pl.when(valid)(outward.wait)
 
 
-def route_kernel(info, fs, pieces, out, table, count):
-    x = info[0]
+def route_kernel(fs, pieces, out, table, count):
+    x = lax.axis_index("x")
     for i in range(2 * F):
         table[i] = 0
     for i in range(F):
@@ -113,12 +115,12 @@
         out[i] = pieces[table[i]]
 
 
-def product_kernel(steps, base, info, fs, mine, theirs, *refs):
+def product_kernel(steps, base, fs, mine, theirs, *refs):
     out, tiles, sems = refs[-3:]
     refs = list(refs[:-3])
-    x, c = info[0], info[3]
-    r = x * 2 + info[1]
-    col = info[2] * 2 + c
+    x, c = lax.axis_index("x"), lax.axis_index("c")
+    r = x * 2 + lax.axis_index("h")
+    col = lax.axis_index(PLANE) * 2 + c
     jobs = []
     for n, step in enumerate(steps):
         k = (x + step) & 3
@@ -161,9 +163,9 @@
             lax.fori_loop(0, loop, body, 0)
 
 
-def homes_kernel(info, fs, *refs):
+def homes_kernel(fs, *refs):
     pieces, out, table, count = refs[:4], refs[4], refs[5], refs[6]
-    x = info[0]
+    x = lax.axis_index("x")
     for i in range(8):
         count[i] = 0
     for p in range(F):
@@ -184,25 +186,33 @@
                     out[F + p] = piece
 
 
-def strip_kernel(info, fs, pieces, panel, strip, upper, keep, send, tmp):
-    h, c = info[1], info[3]
+def strip_kernel(fs, pieces, panels, strip, upper, keep, send, tmp, panel, sems):
+    x = lax.axis_index("x")
+    fetch = pltpu.make_async_copy(panels.at[x, 0], panel, sems.at[0])
+    fetch.start()
+    h, c = lax.axis_index("h"), lax.axis_index("c")
     parts = [pieces[:, ch].reshape(S, HALF) for ch in range(2)]
     value = jnp.concatenate(parts, axis=1)
     strip[...] = -value
-    upper[0, 0] = -value
-    tmp[...] = dot3(split(panel[0, 0]), split(value), ((0,), (0,)))
+    store = pltpu.make_async_copy(strip, upper.at[x, 0], sems.at[1])
+    store.start()
+    fetch.wait()
+    tmp[...] = dot3(split(panel[...]), split(value), ((0,), (0,)))
     for xx in range(4):
         low = pl.multiple_of((xx * 2 + h) * 64, 64)
         for out, ch in ((keep, c), (send, 1 - c)):
             lanes = pl.multiple_of(ch * HALF, HALF)
-            out[:, xx] = tmp[pl.ds(low, 64), pl.ds(lanes, HALF)].reshape(8, 8, HALF)
+            out[xx] = tmp[pl.ds(low, 64), pl.ds(lanes, HALF)].reshape(8, 8, HALF)
+    store.wait()
 
 
 VMEM = pl.BlockSpec(memory_space=pltpu.VMEM)
 ANY = pl.BlockSpec(memory_space=pl.ANY)
-
-
-def call(kernel, info, fs, args, out_shapes, in_specs=None, out_specs=None, scratch=(), flops=0):
+SMEM = pl.BlockSpec(memory_space=pltpu.SMEM)
+HBM = pl.BlockSpec(memory_space=pltpu.HBM)
+
+
+def call(kernel, fs, args, out_shapes, in_specs=None, out_specs=None, scratch=(), flops=0, mib=8):
     single = not isinstance(out_shapes, list)
     shapes = [out_shapes] if single else out_shapes
     out_shape = [jax.ShapeDtypeStruct(s, jnp.float32) for s in shapes]
@@ -210,16 +220,12 @@
     return pl.pallas_call(
         kernel,
         out_shape=out_shape[0] if single else out_shape,
-        grid_spec=pltpu.PrefetchScalarGridSpec(
-            num_scalar_prefetch=2,
-            grid=(1,),
-            in_specs=in_specs or [VMEM] * len(args),
-            out_specs=out_specs or (VMEM if single else [VMEM] * len(shapes)),
-            scratch_shapes=list(scratch),
-        ),
-        compiler_params=pltpu.CompilerParams(vmem_limit_bytes=LIMIT),
+        in_specs=[SMEM, *(in_specs or [VMEM] * len(args))],
+        out_specs=out_specs or (VMEM if single else [VMEM] * len(shapes)),
+        scratch_shapes=list(scratch),
+        compiler_params=pltpu.CompilerParams(vmem_limit_bytes=mib * 1024 * 1024),
         cost_estimate=pl.CostEstimate(flops=flops, bytes_accessed=2 * moved, transcendentals=0),
-    )(info, fs, *args)
+    )(fs, *args)
 
 
 def hop(value, axis, shift):
@@ -241,23 +247,24 @@
 
 
 def local(ancestor, panels, diag_inverse, fs):
-    x, h, c = lax.axis_index("x"), lax.axis_index("h"), lax.axis_index("c")
-    info = jnp.stack([x, h, lax.axis_index(PLANE), c]).astype(jnp.int32)
-    own_panel = pl.BlockSpec((1, 1, S, W), lambda i, info, fs: (info[0], 0, 0, 0))
-
-    packed = call(pack_kernel, info, fs, [panels], (8, 2, FRONT, HALF), in_specs=[own_panel])
+    x, c = lax.axis_index("x"), lax.axis_index("c")
+    packed = call(
+        pack_kernel, fs, [panels], (8, 2, FRONT, HALF), in_specs=[HBM],
+        scratch=[pltpu.VMEM((S, W), jnp.float32), pltpu.SemaphoreType.DMA], mib=60,
+    )
     pieces = exchange(packed.reshape(F, FRONT, HALF), COL)
     routed = call(
-        route_kernel, info, fs, [pieces], (2 * F, FRONT, HALF),
+        route_kernel, fs, [pieces], (2 * F, FRONT, HALF),
         scratch=[pltpu.SMEM((2 * F,), jnp.int32), pltpu.SMEM((F,), jnp.int32)],
     )
     panel = exchange(routed.reshape(8, 4, FRONT, HALF), PLANE)
     first_tiles, rest_tiles = call(
-        gather_kernel, info, fs, [ancestor, packed], [(1, 2, 4, S, S), (3, 2, 4, S, S)],
-        in_specs=[ANY, ANY], out_specs=[ANY, ANY],
+        gather_kernel, fs, [ancestor, packed], [(1, 2, 4, S, S), (3, 2, 4, S, S)],
+        in_specs=[HBM, ANY], out_specs=[HBM, HBM],
         scratch=[pltpu.VMEM((K, 4, 2, S, S), jnp.float32),
                  pltpu.SMEM((K * 8,), jnp.int32), pltpu.SMEM((K * 4,), jnp.int32),
                  pltpu.SemaphoreType.DMA((K, 4, 2)), pltpu.SemaphoreType.DMA((K, 4, 2))],
+        mib=60,
     )
     first_pair = [first_tiles, hop(first_tiles, "c", 1)]
     rest_pair = [rest_tiles, hop(rest_tiles, "c", 1)]
@@ -266,18 +273,18 @@
     def product(steps, base, pair, blocks, behind=()):
         n = len(steps)
         return call(
-            functools.partial(product_kernel, steps, base), info, fs,
+            functools.partial(product_kernel, steps, base), fs,
             [*pair, *blocks, *behind], (16, n, 4, PIECE, HALF),
-            in_specs=[ANY] * 2 + [VMEM] * len(blocks) + [ANY] * len(behind),
+            in_specs=[HBM] * 2 + [VMEM] * len(blocks) + [ANY] * len(behind),
             scratch=[pltpu.VMEM((n, 2, 2, 4, S, S), jnp.float32),
                      pltpu.SemaphoreType.DMA((n, 2, 2, 4))],
-            flops=n * 10**9,
+            flops=n * 10**9, mib=8 * n + 6,
         )
 
     def total(value):
         value = exchange(value, SHEET)
-        value = value.reshape(2, 8, *value.shape[1:]).sum(1)
-        return [value[:, n] for n in range(value.shape[1])]
+        value = value.reshape(2, 8, *value.shape[1:])
+        return [value[:, :, n].sum(1) for n in range(value.shape[2])]
 
     own_product = product((0,), 0, first_pair, [panel])
     (own,) = total(own_product)
@@ -288,19 +295,21 @@
     (far,) = total(far_product)
     sources = [own, hop(near[0], "x", -1), hop(far, "x", 2), hop(near[1], "x", 1)]
     homes = call(
-        homes_kernel, info, fs, sources, (2 * F, PIECE, HALF),
+        homes_kernel, fs, sources, (2 * F, PIECE, HALF),
         scratch=[pltpu.SMEM((32,), jnp.int32), pltpu.SMEM((8,), jnp.int32)],
     )
     placed = exchange(homes, ("h", *COL)).reshape(16, 2, PIECE, HALF)
     strip, upper, part, part_send = call(
-        strip_kernel, info, fs, [placed, panels],
-        [(S, W), (K, 1, S, W), (8, 4, 8, HALF), (8, 4, 8, HALF)], in_specs=[VMEM, own_panel],
-        out_specs=[VMEM, own_panel, VMEM, VMEM],
-        scratch=[pltpu.VMEM((W, W), jnp.float32)],
+        strip_kernel, fs, [placed, panels],
+        [(S, W), (K, 1, S, W), (4, 8, 8, HALF), (4, 8, 8, HALF)], in_specs=[VMEM, HBM],
+        out_specs=[VMEM, HBM, VMEM, VMEM],
+        scratch=[pltpu.VMEM((W, W), jnp.float32), pltpu.VMEM((S, W), jnp.float32),
+                 pltpu.SemaphoreType.DMA((2,))],
     )
     before, after, top, bottom = gather_x(strip)
-    part = exchange(part + hop(part_send, "c", 1), PLANE).sum(0)
-    part = exchange(part, ("x",))
+    part = (part + hop(part_send, "c", 1)).reshape(32, 8, HALF)
+    part = exchange(part, ("x", *PLANE))
+    part = part.reshape(4, 8, 8, HALF).sum(1)
     part = exchange(jnp.broadcast_to(part[None], (8, *part.shape)), PLANE)
     for value, step, low in ((before, 3, 0), (after, 1, 0), (top, 2, 0), (bottom, 2, S // 2)):
         k = (x + step) & 3

time: 218 us -> 205 us (0.940)
  Pallas kernels: 36.1 us -> 24.6 us
  blocking collectives: 66.2 us -> 55.9 us
  waiting for transfers between devices: 57.3 us -> 65.1 us
    pallas_call x8, Pallas kernels: 36.1 us -> 24.6 us  [call(): pl.pallas_call(kernel, out_shape=out_shape[0] if single else out_shape, i...]
    all_to_all x4 -> x3, blocking collectives: 66.2 us -> 55.9 us  [exchange(): return lax.all_to_all(value, axes, 0, 0, tiled=True)]
    all_to_all x5, waiting for transfers between devices: 32.8 us -> 40.4 us  [exchange(): return lax.all_to_all(value, axes, 0, 0, tiled=True)]
    reduce_sum x4, other arithmetic: 1.63 us -> 4.41 us  [the longest x3 4.4 us: total(): return [value[:, :, n].sum(1) for n in range(value.shape[2])]]
    unnamed x22 -> x14, local copies, waits for them, and re-layouts: 4.47 us -> 5.6 us
  transfers between devices with their start and end apart: 20 -> 20, of which waited for: 11 -> 9; matrix products, arithmetic and copies ran while one was open for 3% -> 4% of each run, Pallas kernels for 6% -> 3%
where the time goes in v1:
time: 205 us; the launch traced here: 204 us
  waiting for transfers between devices  65.1 us (32%)
  blocking collectives  55.9 us (27%)
  starting transfers between devices  41.8 us (20%)
  Pallas kernels  24.6 us (12%)
  local copies, waits for them, and re-layouts  9.56 us (5%)
  other arithmetic  6.06 us (3%)
    all_to_all x3, blocking collectives, exchange(): return lax.all_to_all(value, axes, 0, 0, tiled=True)  55.9 us
    all_to_all x5, waiting for transfers between devices, exchange(): return lax.all_to_all(value, axes, 0, 0, tiled=True)  40.4 us
    ppermute x15, waiting for transfers between devices, hop(): lax.ppermute(value, axis, [(i, (i + shift) % size) for i in range(size)])  24.7 us
    pallas_call x8, Pallas kernels, call(): pl.pallas_call(kernel, out_shape=out_shape[0] if single else out_shape, i...  24.6 us
    all_to_all x5, starting transfers between devices, exchange(): return lax.all_to_all(value, axes, 0, 0, tiled=True)  22.8 us
    ppermute x15, starting transfers between devices, hop(): lax.ppermute(value, axis, [(i, (i + shift) % size) for i in range(size)])  18.9 us
    unnamed x14, local copies, waits for them, and re-layouts  5.6 us
    reduce_sum x3, other arithmetic, total(): return [value[:, :, n].sum(1) for n in range(value.shape[2])]  4.4 us
  transfers between devices with their start and end apart: 20, of which 9 were waited for; matrix products, arithmetic and copies ran while one was open for 4% of the time, Pallas kernels for 3%

profile of v1, /device:TPU:1, one launch (start us, length us, event | category | flops | bytes accessed | tf_op | source)
XLA Modules:
  0.0 203.9 jit_solution(8991511544794505606)
XLA Ops:
  0.6 2.6 %shard_map.59.after = f32[8,2,32,256]{3,2,1,0:T(8,128)} custom-call(s32[4,16]{1,0:T(4,128)} %fs.15, f32[4,1,256,512]{3,2,1,0:T(8,128)} %panels.3), custom_call_target="tpu_custom_call" | custom-call | bytes 1048576 | tf_op jit(solution)/shard_map/pallas_call | solution.py:220
  3.2 4.6 %shard_map.60 = (f32[1,2,4,256,256]{4,3,2,1,0:T(8,128)}, f32[3,2,4,256,256]{4,3,2,1,0:T(8,128)}) custom-call(s32[4,16]{1,0:T(4,128)} %fs.15, f32[3072,1536]{1,0:T(8,128)} %ancestor.1, f32[8,2,32,256]{3,2,1,0:T(8,128)} %shard_map.59.after), custom_call_target="tpu_custom_call" | custom-call | bytes 16777216 | tf_op jit(solution)/shard_map/pallas_call | solution.py:220
  7.8 1.2 collective-permute-start.1
  9.1 16.1 %all_to_all.40.pieces = f32[16,32,256]{2,1,0:T(8,128)S(1)} all-to-all(f32[16,32,256]{2,1,0:T(8,128)S(1)} %bitcast.28), channel_id=1, replica_groups=mesh['x'=4,'h'=2,'l'=2,'z'=4,'c'=2] {'l','z','c'}, dimensions={0} | all-to-all | bytes 1048576 | tf_op jit(solution)/shard_map/all_to_all | solution.py:237
  25.2 0.7 shard_map.61
  26.0 17.5 %all_to_all.41.refs_0_ = f32[8,4,32,256]{3,2,1,0:T(8,128)S(1)} all-to-all(f32[8,4,32,256]{3,2,1,0:T(8,128)S(1)} %bitcast.26), channel_id=1, replica_groups=mesh['x'=4,'h'=2,'l'=2,'z'=4,'c'=2] {'l','z'}, dimensions={0} | all-to-all | bytes 2097152 | tf_op jit(solution)/shard_map/all_to_all | solution.py:237
  43.5 2.2 %shard_map.62 = f32[16,1,4,16,256]{4,3,2,1,0:T(8,128)} custom-call(s32[4,16]{1,0:T(4,128)S(1)} %copy-done.4, f32[1,2,4,256,256]{4,3,2,1,0:T(8,128)S(1)} %copy-done.3, f32[1,2,4,256,256]{4,3,2,1,0:T(8,128)S(1)} %collective-permute-done.theirs, f32[8,4,32,256]{3,2,1,0:T(8,128)S(1)} %all_to_all.41.refs_0_), custom_call_target="tpu_custom_call" | custom-call | flops 1000000000 | bytes 2097152 | tf_op jit(solution)/shard_map/pallas_call | solution.py:220
  45.7 5.4 %all-to-all-start.2 = ((f32[16,1,4,16,256]{4,3,2,1,0:T(8,128)}), f32[16,1,4,16,256]{4,3,2,1,0:T(8,128)}, u32[]{:S(2)}, u32[]{:S(2)}) async-start(f32[16,1,4,16,256]{4,3,2,1,0:T(8,128)} %shard_map.62), calls=%async_computation.2 | async-start | bytes 2097152 | tf_op jit(solution)/shard_map/all_to_all | solution.py:237
  51.2 3.2 %collective-permute-start.2 = (f32[8,4,32,256]{3,2,1,0:T(8,128)S(1)}, f32[8,4,32,256]{3,2,1,0:T(8,128)S(1)}, u32[]{:S(2)}, u32[]{:S(2)}) collective-permute-start(f32[8,4,32,256]{3,2,1,0:T(8,128)S(1)} %all_to_all.41.refs_0_), channel_id=1, source_target_pairs={{0,32},{32,64},{64,96},{96,0},{1,33},{33,65},{65,97},{97,1},{2,34}... | collective-permute-start | bytes 3145736 | tf_op jit(solution)/shard_map/ppermute | solution.py:233
  54.4 0.9 collective-permute-start.3
  55.3 11.0 %all-to-all-done.2 = f32[16,1,4,16,256]{4,3,2,1,0:T(8,128)} async-done(((f32[16,1,4,16,256]{4,3,2,1,0:T(8,128)}), f32[16,1,4,16,256]{4,3,2,1,0:T(8,128)}, u32[]{:S(2)}, u32[]{:S(2)}) %all-to-all-start.2) | async-done | bytes 1048608 | tf_op jit(solution)/shard_map/all_to_all | solution.py:237
  66.3 1.3 bitcast_reduce_fusion.1.refs_2_.refs_0_
  67.6 8.7 %collective-permute-done.2.refs_0_ = f32[8,4,32,256]{3,2,1,0:T(8,128)S(1)} collective-permute-done((f32[8,4,32,256]{3,2,1,0:T(8,128)S(1)}, f32[8,4,32,256]{3,2,1,0:T(8,128)S(1)}, u32[]{:S(2)}, u32[]{:S(2)}) %collective-permute-start.2) | collective-permute-done | bytes 1048608 | tf_op jit(solution)/shard_map/ppermute | solution.py:233
  76.3 1.2 collective-permute-done.3.refs_1_
  77.5 2.8 %copy-done = f32[3,2,4,256,256]{4,3,2,1,0:T(8,128)S(1)} copy-done((f32[3,2,4,256,256]{4,3,2,1,0:T(8,128)S(1)}, f32[3,2,4,256,256]{4,3,2,1,0:T(8,128)}, u32[]{:S(2)}) %copy-start) | copy-done | bytes 6291480
  80.2 8.7 %shard_map.63.refs_2_ = f32[16,2,4,16,256]{4,3,2,1,0:T(8,128)} custom-call(s32[4,16]{1,0:T(4,128)S(1)} %copy-done.4, f32[3,2,4,256,256]{4,3,2,1,0:T(8,128)S(1)} %copy-done, f32[3,2,4,256,256]{4,3,2,1,0:T(8,128)} %collective-permute-done.1.theirs, f32[8,4,32,256]{3,2,1,0:T(8,128)S(1)} %collective-permute-done.2.refs_0_, ...), custom_call_target="tpu_custom_call" | custom-call | flops 2000000000 | bytes 4194304 | tf_op jit(solution)/shard_map/pallas_call | solution.py:220
  88.9 4.5 %all-to-all-start.3 = ((f32[16,2,4,16,256]{4,3,2,1,0:T(8,128)}), f32[16,2,4,16,256]{4,3,2,1,0:T(8,128)}, u32[]{:S(2)}, u32[]{:S(2)}) async-start(f32[16,2,4,16,256]{4,3,2,1,0:T(8,128)} %shard_map.63.refs_2_), calls=%async_computation.3 | async-start | bytes 4194304 | tf_op jit(solution)/shard_map/all_to_all | solution.py:237
  93.5 1.0 collective-permute-start.4
  94.5 1.8 collective-permute-start.5
  96.3 9.5 %collective-permute-done.4.refs_0_ = f32[4,4,32,256]{3,2,1,0:T(8,128)S(1)} collective-permute-done((f32[4,4,32,256]{3,2,1,0:T(8,128)S(1)}, f32[4,4,32,256]{3,2,1,0:T(8,128)S(1)}, u32[]{:S(2)}, u32[]{:S(2)}) %collective-permute-start.4) | collective-permute-done | bytes 524320 | tf_op jit(solution)/shard_map/ppermute | solution.py:233
  105.8 2.8 %copy-done.1 = f32[3,2,4,256,256]{4,3,2,1,0:T(8,128)S(1)} copy-done((f32[3,2,4,256,256]{4,3,2,1,0:T(8,128)S(1)}, f32[3,2,4,256,256]{4,3,2,1,0:T(8,128)}, u32[]{:S(2)}) %copy-start.1) | copy-done | bytes 6291480
  108.6 3.4 %shard_map.64 = f32[16,1,4,16,256]{4,3,2,1,0:T(8,128)} custom-call(s32[4,16]{1,0:T(4,128)S(1)} %copy-done.4, f32[3,2,4,256,256]{4,3,2,1,0:T(8,128)S(1)} %copy-done.1, f32[3,2,4,256,256]{4,3,2,1,0:T(8,128)} %collective-permute-done.1.theirs, f32[4,4,32,256]{3,2,1,0:T(8,128)S(1)} %collective-permute-done.4.refs_0_, ...), custom_call_target="tpu_custom_call" | custom-call | flops 1000000000 | bytes 2097152 | tf_op jit(solution)/shard_map/pallas_call | solution.py:220
  112.0 7.2 %all-to-all-done.3 = f32[16,2,4,16,256]{4,3,2,1,0:T(8,128)} async-done(((f32[16,2,4,16,256]{4,3,2,1,0:T(8,128)}), f32[16,2,4,16,256]{4,3,2,1,0:T(8,128)}, u32[]{:S(2)}, u32[]{:S(2)}) %all-to-all-start.3) | async-done | bytes 2097184 | tf_op jit(solution)/shard_map/all_to_all | solution.py:237
  119.1 1.8 slice_reduce_fusion
  120.9 5.7 %all-to-all-start.4 = ((f32[16,1,4,16,256]{4,3,2,1,0:T(8,128)}), f32[16,1,4,16,256]{4,3,2,1,0:T(8,128)}, u32[]{:S(2)}, u32[]{:S(2)}) async-start(f32[16,1,4,16,256]{4,3,2,1,0:T(8,128)} %shard_map.64), calls=%async_computation.4 | async-start | bytes 2097152 | tf_op jit(solution)/shard_map/all_to_all | solution.py:237
  126.6 0.4 collective-permute-start.6
  127.0 1.3 collective-permute-start.8
  128.3 10.3 %all-to-all-done.4 = f32[16,1,4,16,256]{4,3,2,1,0:T(8,128)} async-done(((f32[16,1,4,16,256]{4,3,2,1,0:T(8,128)}), f32[16,1,4,16,256]{4,3,2,1,0:T(8,128)}, u32[]{:S(2)}, u32[]{:S(2)}) %all-to-all-start.4) | async-done | bytes 1048608 | tf_op jit(solution)/shard_map/all_to_all | solution.py:237
  138.6 1.3 bitcast_reduce_fusion
  140.0 5.3 %collective-permute-done.7.refs_2_ = f32[2,4,16,256]{3,2,1,0:T(8,128)S(1)} collective-permute-done((f32[2,4,16,256]{3,2,1,0:T(8,128)S(1)}, f32[2,4,16,256]{3,2,1,0:T(8,128)S(1)}, u32[]{:S(2)}, u32[]{:S(2)}) %collective-permute-start.7) | collective-permute-done | bytes 131104 | tf_op jit(solution)/shard_map/ppermute | solution.py:233
  145.3 1.0 shard_map.65
  146.3 22.3 %all_to_all.42 = f32[32,16,256]{2,1,0:T(8,128)S(1)} all-to-all(f32[32,16,256]{2,1,0:T(8,128)S(1)} %shard_map.65), channel_id=1, replica_groups=mesh['x'=4,'h'=2,'l'=2,'z'=4,'c'=2] {'h','l','z','c'}, dimensions={0} | all-to-all | bytes 1048576 | tf_op jit(solution)/shard_map/all_to_all | solution.py:237
  168.6 1.5 shard_map.66
  170.2 1.6 collective-permute-start.9
  171.8 1.1 collective-permute-start.10
  172.9 0.7 add.32
  173.6 3.9 %all-to-all-start.6 = ((f32[32,8,256]{2,1,0:T(8,128)}), f32[32,8,256]{2,1,0:T(8,128)S(1)}, u32[]{:S(2)}, u32[]{:S(2)}) async-start(f32[32,8,256]{2,1,0:T(8,128)} %bitcast.10), calls=%async_computation.6 | async-start | bytes 524288 | tf_op jit(solution)/shard_map/all_to_all | solution.py:237
  177.5 10.5 %all-to-all-done.6 = f32[32,8,256]{2,1,0:T(8,128)S(1)} async-done(((f32[32,8,256]{2,1,0:T(8,128)}), f32[32,8,256]{2,1,0:T(8,128)S(1)}, u32[]{:S(2)}, u32[]{:S(2)}) %all-to-all-start.6) | async-done | bytes 262176 | tf_op jit(solution)/shard_map/all_to_all | solution.py:237
  188.0 0.7 broadcast_in_dim.22
  188.7 3.4 %all-to-all-start.7 = ((f32[8,4,8,256]{3,2,1,0:T(8,128)}), f32[8,4,8,256]{3,2,1,0:T(8,128)S(1)}, u32[]{:S(2)}, u32[]{:S(2)}) async-start(f32[8,4,8,256]{3,2,1,0:T(8,128)} %broadcast_in_dim.22), calls=%async_computation.7 | async-start | bytes 524288 | tf_op jit(solution)/shard_map/all_to_all | solution.py:237
  192.5 2.5 %collective-permute-start.12 = (f32[128,512]{1,0:T(8,128)S(1)}, f32[128,512]{1,0:T(8,128)S(1)}, u32[]{:S(2)}, u32[]{:S(2)}) collective-permute-start(f32[128,512]{1,0:T(8,128)S(1)} %slice.29), channel_id=1, source_target_pairs={{0,96},{32,0},{64,32},{96,64},{1,97},{33,1},{65,33},{97,65},{2,98}... | collective-permute-start | bytes 786440 | tf_op jit(solution)/shard_map/ppermute | solution.py:233
  195.0 0.8 bitcast_dynamic-update-slice_fusion.1
  195.9 0.8 bitcast_dynamic-update-slice_fusion
  196.7 1.5 all-to-all-done.7
  198.2 3.3 %collective-permute-start.14 = (f32[4,64,256]{2,1,0:T(8,128)S(1)}, f32[4,64,256]{2,1,0:T(8,128)S(1)}, u32[]{:S(2)}, u32[]{:S(2)}) collective-permute-start(f32[4,64,256]{2,1,0:T(8,128)S(1)} %bitcast.29), channel_id=1, source_target_pairs={{0,1},{1,0},{2,3},{3,2},{4,5},{5,4},{6,7},{7,6},{8,9},{9,8},{10,11... | collective-permute-start | bytes 786440 | tf_op jit(solution)/shard_map/ppermute | solution.py:233
  201.6 0.7 bitcast_dynamic-update-slice_fusion.3
  202.3 0.7 bitcast_dynamic-update-slice_fusion.2
  203.0 0.9 fusion
  (33 shorter events, 0.8 us)
Async XLA Ops:
  3.2 5.9 %copy-start.5 = (f32[8,2,32,256]{3,2,1,0:T(8,128)S(1)}, f32[8,2,32,256]{3,2,1,0:T(8,128)}, u32[]{:S(2)}) copy-start(f32[8,2,32,256]{3,2,1,0:T(8,128)} %shard_map.59.after) | copy-start | bytes 1572868
  3.2 22.0 %copy-start.4 = (s32[4,16]{1,0:T(4,128)S(1)}, s32[4,16]{1,0:T(4,128)}, u32[]{:S(2)}) copy-start(s32[4,16]{1,0:T(4,128)} %fs.15) | copy-start | bytes 772
  7.8 69.6 %collective-permute-start.1 = (f32[3,2,4,256,256]{4,3,2,1,0:T(8,128)}, f32[3,2,4,256,256]{4,3,2,1,0:T(8,128)}, u32[]{:S(2)}, u32[]{:S(2)}) collective-permute-start(f32[3,2,4,256,256]{4,3,2,1,0:T(8,128)} %get-tuple-element.12.mine), channel_id=1, source_target_pairs={{0,1},{1,0},{2,3},{3,2},{4,5},{5,4},{6,7},{7,6},{8,9},{9,8},{10,11... | collective-permute-start | bytes 18874376 | tf_op jit(solution)/shard_map/ppermute | solution.py:233
  9.0 34.5 %collective-permute-start = (f32[1,2,4,256,256]{4,3,2,1,0:T(8,128)}, f32[1,2,4,256,256]{4,3,2,1,0:T(8,128)S(1)}, u32[]{:S(2)}, u32[]{:S(2)}) collective-permute-start(f32[1,2,4,256,256]{4,3,2,1,0:T(8,128)} %get-tuple-element.11.mine), channel_id=1, source_target_pairs={{0,1},{1,0},{2,3},{3,2},{4,5},{5,4},{6,7},{7,6},{8,9},{9,8},{10,11... | collective-permute-start | bytes 6291464 | tf_op jit(solution)/shard_map/ppermute | solution.py:233
  25.2 18.2 %copy-start.3 = (f32[1,2,4,256,256]{4,3,2,1,0:T(8,128)S(1)}, f32[1,2,4,256,256]{4,3,2,1,0:T(8,128)}, u32[]{:S(2)}) copy-start(f32[1,2,4,256,256]{4,3,2,1,0:T(8,128)} %get-tuple-element.11.mine) | copy-start | bytes 6291460
  45.7 20.5 %all-to-all-start.2 = ((f32[16,1,4,16,256]{4,3,2,1,0:T(8,128)}), f32[16,1,4,16,256]{4,3,2,1,0:T(8,128)}, u32[]{:S(2)}, u32[]{:S(2)}) async-start(f32[16,1,4,16,256]{4,3,2,1,0:T(8,128)} %shard_map.62), calls=%async_computation.2 | async-start | bytes 2097152 | tf_op jit(solution)/shard_map/all_to_all | solution.py:237
  51.2 25.1 %collective-permute-start.2 = (f32[8,4,32,256]{3,2,1,0:T(8,128)S(1)}, f32[8,4,32,256]{3,2,1,0:T(8,128)S(1)}, u32[]{:S(2)}, u32[]{:S(2)}) collective-permute-start(f32[8,4,32,256]{3,2,1,0:T(8,128)S(1)} %all_to_all.41.refs_0_), channel_id=1, source_target_pairs={{0,32},{32,64},{64,96},{96,0},{1,33},{33,65},{65,97},{97,1},{2,34}... | collective-permute-start | bytes 3145736 | tf_op jit(solution)/shard_map/ppermute | solution.py:233
  54.4 23.1 %collective-permute-start.3 = (f32[8,4,32,256]{3,2,1,0:T(8,128)S(1)}, f32[8,4,32,256]{3,2,1,0:T(8,128)S(1)}, u32[]{:S(2)}, u32[]{:S(2)}) collective-permute-start(f32[8,4,32,256]{3,2,1,0:T(8,128)S(1)} %all_to_all.41.refs_0_), channel_id=1, source_target_pairs={{0,96},{32,0},{64,32},{96,64},{1,97},{33,1},{65,33},{97,65},{2,98}... | collective-permute-start | bytes 3145736 | tf_op jit(solution)/shard_map/ppermute | solution.py:233
  77.5 2.8 %copy-start = (f32[3,2,4,256,256]{4,3,2,1,0:T(8,128)S(1)}, f32[3,2,4,256,256]{4,3,2,1,0:T(8,128)}, u32[]{:S(2)}) copy-start(f32[3,2,4,256,256]{4,3,2,1,0:T(8,128)} %get-tuple-element.12.mine) | copy-start | bytes 18874372
  88.9 30.2 %all-to-all-start.3 = ((f32[16,2,4,16,256]{4,3,2,1,0:T(8,128)}), f32[16,2,4,16,256]{4,3,2,1,0:T(8,128)}, u32[]{:S(2)}, u32[]{:S(2)}) async-start(f32[16,2,4,16,256]{4,3,2,1,0:T(8,128)} %shard_map.63.refs_2_), calls=%async_computation.3 | async-start | bytes 4194304 | tf_op jit(solution)/shard_map/all_to_all | solution.py:237
  93.5 12.3 %collective-permute-start.4 = (f32[4,4,32,256]{3,2,1,0:T(8,128)S(1)}, f32[4,4,32,256]{3,2,1,0:T(8,128)S(1)}, u32[]{:S(2)}, u32[]{:S(2)}) collective-permute-start(f32[4,4,32,256]{3,2,1,0:T(8,128)S(1)} %slice.26), channel_id=1, source_target_pairs={{0,32},{32,64},{64,96},{96,0},{1,33},{33,65},{65,97},{97,1},{2,34}... | collective-permute-start | bytes 1572872 | tf_op jit(solution)/shard_map/ppermute | solution.py:233
  94.5 11.3 %collective-permute-start.5 = (f32[4,4,32,256]{3,2,1,0:T(8,128)S(1)}, f32[4,4,32,256]{3,2,1,0:T(8,128)S(1)}, u32[]{:S(2)}, u32[]{:S(2)}) collective-permute-start(f32[4,4,32,256]{3,2,1,0:T(8,128)S(1)} %slice.27), channel_id=1, source_target_pairs={{0,96},{32,0},{64,32},{96,64},{1,97},{33,1},{65,33},{97,65},{2,98}... | collective-permute-start | bytes 1572872 | tf_op jit(solution)/shard_map/ppermute | solution.py:233
  105.8 2.8 %copy-start.1 = (f32[3,2,4,256,256]{4,3,2,1,0:T(8,128)S(1)}, f32[3,2,4,256,256]{4,3,2,1,0:T(8,128)}, u32[]{:S(2)}) copy-start(f32[3,2,4,256,256]{4,3,2,1,0:T(8,128)} %get-tuple-element.12.mine) | copy-start | bytes 18874372
  120.9 17.7 %all-to-all-start.4 = ((f32[16,1,4,16,256]{4,3,2,1,0:T(8,128)}), f32[16,1,4,16,256]{4,3,2,1,0:T(8,128)}, u32[]{:S(2)}, u32[]{:S(2)}) async-start(f32[16,1,4,16,256]{4,3,2,1,0:T(8,128)} %shard_map.64), calls=%async_computation.4 | async-start | bytes 2097152 | tf_op jit(solution)/shard_map/all_to_all | solution.py:237
  126.6 42.0 %copy-start.2 = (f32[4,1,256,512]{3,2,1,0:T(8,128)S(1)}, f32[4,1,256,512]{3,2,1,0:T(8,128)}, u32[]{:S(2)}) copy-start(f32[4,1,256,512]{3,2,1,0:T(8,128)} %panels.3) | copy-start | bytes 6291460
  126.6 13.4 %collective-permute-start.6 = (f32[2,4,16,256]{3,2,1,0:T(8,128)S(1)}, f32[2,4,16,256]{3,2,1,0:T(8,128)S(1)}, u32[]{:S(2)}, u32[]{:S(2)}) collective-permute-start(f32[2,4,16,256]{3,2,1,0:T(8,128)S(1)} %get-tuple-element.13), channel_id=1, source_target_pairs={{0,96},{32,0},{64,32},{96,64},{1,97},{33,1},{65,33},{97,65},{2,98}... | collective-permute-start | bytes 393224 | tf_op jit(solution)/shard_map/ppermute | solution.py:233
  127.0 13.0 %collective-permute-start.8 = (f32[2,4,16,256]{3,2,1,0:T(8,128)S(1)}, f32[2,4,16,256]{3,2,1,0:T(8,128)S(1)}, u32[]{:S(2)}, u32[]{:S(2)}) collective-permute-start(f32[2,4,16,256]{3,2,1,0:T(8,128)S(1)} %get-tuple-element.15), channel_id=1, source_target_pairs={{0,32},{32,64},{64,96},{96,0},{1,33},{33,65},{65,97},{97,1},{2,34}... | collective-permute-start | bytes 393224 | tf_op jit(solution)/shard_map/ppermute | solution.py:233
  139.9 5.4 %collective-permute-start.7 = (f32[2,4,16,256]{3,2,1,0:T(8,128)S(1)}, f32[2,4,16,256]{3,2,1,0:T(8,128)S(1)}, u32[]{:S(2)}, u32[]{:S(2)}) collective-permute-start(f32[2,4,16,256]{3,2,1,0:T(8,128)S(1)} %bitcast_reduce_fusion), channel_id=1, source_target_pairs={{0,64},{32,96},{64,0},{96,32},{1,65},{33,97},{65,1},{97,33},{2,66}... | collective-permute-start | bytes 393224 | tf_op jit(solution)/shard_map/ppermute | solution.py:233
  170.1 2.8 %collective-permute-start.13 = (f32[4,8,8,256]{3,2,1,0:T(8,128)S(1)}, f32[4,8,8,256]{3,2,1,0:T(8,128)S(1)}, u32[]{:S(2)}, u32[]{:S(2)}) collective-permute-start(f32[4,8,8,256]{3,2,1,0:T(8,128)S(1)} %get-tuple-element.19), channel_id=1, source_target_pairs={{0,1},{1,0},{2,3},{3,2},{4,5},{5,4},{6,7},{7,6},{8,9},{9,8},{10,11... | collective-permute-start | bytes 786440 | tf_op jit(solution)/shard_map/ppermute | solution.py:233
  170.2 22.0 %collective-permute-start.9 = (f32[256,512]{1,0:T(8,128)S(1)}, f32[256,512]{1,0:T(8,128)S(1)}, u32[]{:S(2)}, u32[]{:S(2)}) collective-permute-start(f32[256,512]{1,0:T(8,128)S(1)} %get-tuple-element.17), channel_id=1, source_target_pairs={{0,32},{32,64},{64,96},{96,0},{1,33},{33,65},{65,97},{97,1},{2,34}... | collective-permute-start | bytes 1572872 | tf_op jit(solution)/shard_map/ppermute | solution.py:233
  171.8 20.7 %collective-permute-start.10 = (f32[256,512]{1,0:T(8,128)S(1)}, f32[256,512]{1,0:T(8,128)S(1)}, u32[]{:S(2)}, u32[]{:S(2)}) collective-permute-start(f32[256,512]{1,0:T(8,128)S(1)} %get-tuple-element.17), channel_id=1, source_target_pairs={{0,96},{32,0},{64,32},{96,64},{1,97},{33,1},{65,33},{97,65},{2,98}... | collective-permute-start | bytes 1572872 | tf_op jit(solution)/shard_map/ppermute | solution.py:233
  173.6 14.3 %all-to-all-start.6 = ((f32[32,8,256]{2,1,0:T(8,128)}), f32[32,8,256]{2,1,0:T(8,128)S(1)}, u32[]{:S(2)}, u32[]{:S(2)}) async-start(f32[32,8,256]{2,1,0:T(8,128)} %bitcast.10), calls=%async_computation.6 | async-start | bytes 524288 | tf_op jit(solution)/shard_map/all_to_all | solution.py:237
  188.7 9.5 %all-to-all-start.7 = ((f32[8,4,8,256]{3,2,1,0:T(8,128)}), f32[8,4,8,256]{3,2,1,0:T(8,128)S(1)}, u32[]{:S(2)}, u32[]{:S(2)}) async-start(f32[8,4,8,256]{3,2,1,0:T(8,128)} %broadcast_in_dim.22), calls=%async_computation.7 | async-start | bytes 524288 | tf_op jit(solution)/shard_map/all_to_all | solution.py:237
  192.2 10.8 %copy-start.6 = (f32[4,64,512]{2,1,0:T(8,128)S(1)}, f32[4,64,512]{2,1,0:T(8,128)}, u32[]{:S(2)}) copy-start(f32[4,64,512]{2,1,0:T(8,128)} %param.6) | copy-start | bytes 1572868
  192.2 9.4 %collective-permute-start.11 = (f32[128,512]{1,0:T(8,128)S(1)}, f32[128,512]{1,0:T(8,128)S(1)}, u32[]{:S(2)}, u32[]{:S(2)}) collective-permute-start(f32[128,512]{1,0:T(8,128)S(1)} %slice.28), channel_id=1, source_target_pairs={{0,32},{32,64},{64,96},{96,0},{1,33},{33,65},{65,97},{97,1},{2,34}... | collective-permute-start | bytes 786440 | tf_op jit(solution)/shard_map/ppermute | solution.py:233
  192.5 9.8 %collective-permute-start.12 = (f32[128,512]{1,0:T(8,128)S(1)}, f32[128,512]{1,0:T(8,128)S(1)}, u32[]{:S(2)}, u32[]{:S(2)}) collective-permute-start(f32[128,512]{1,0:T(8,128)S(1)} %slice.29), channel_id=1, source_target_pairs={{0,96},{32,0},{64,32},{96,64},{1,97},{33,1},{65,33},{97,65},{2,98}... | collective-permute-start | bytes 786440 | tf_op jit(solution)/shard_map/ppermute | solution.py:233
  198.2 4.8 %collective-permute-start.14 = (f32[4,64,256]{2,1,0:T(8,128)S(1)}, f32[4,64,256]{2,1,0:T(8,128)S(1)}, u32[]{:S(2)}, u32[]{:S(2)}) collective-permute-start(f32[4,64,256]{2,1,0:T(8,128)S(1)} %bitcast.29), channel_id=1, source_target_pairs={{0,1},{1,0},{2,3},{3,2},{4,5},{5,4},{6,7},{7,6},{8,9},{9,8},{10,11... | collective-permute-start | bytes 786440 | tf_op jit(solution)/shard_map/ppermute | solution.py:233

commit v2 on v1

--- a/solution.py
+++ b/solution.py
@@ -157,15 +157,21 @@
             def body(i, carry):
                 copy(i).wait()
                 value = dot3(split(tiles[(*spot, i)]), right, ((1,), (0,)))
-                out[:, n, i] += value.reshape(16, PIECE, HALF)
+                if out.shape[0] == 8:
+                    out[:, n, i] += value.reshape(8, FRONT, HALF)
+                else:
+                    value = value.reshape(8, 2, PIECE, HALF)
+                    for h in range(2):
+                        out[h * 8 : h * 8 + 8, n, i] += value[:, h]
                 return carry
 
             lax.fori_loop(0, loop, body, 0)
 
 
 def homes_kernel(fs, *refs):
-    pieces, out, table, count = refs[:4], refs[4], refs[5], refs[6]
-    x = lax.axis_index("x")
+    own, arrived, far, out, table, count = refs
+    pieces = [own, *(arrived.at[n] for n in range(5))]
+    x, h = lax.axis_index("x"), lax.axis_index("h")
     for i in range(8):
         count[i] = 0
     for p in range(F):
@@ -173,17 +179,19 @@
         n = count[r]
         table[r * 4 + jnp.minimum(n, 3)] = p
         count[r] = n + 1
-    for dx in range(4):
-        for h in range(2):
-            r = ((x + dx) & 3) * 2 + h
-            for i in range(4):
-
-                @pl.when(i < count[r])
-                def _():
-                    p = table[r * 4 + i]
-                    piece = pieces[dx][h, i]
-                    out[p] = piece
-                    out[F + p] = piece
+    sources = [(((x + 2) & 3) * 2 + hs, far.at[hs]) for hs in range(2)]
+    for n, dx in enumerate((0, 1, 3)):
+        for dh in range(2):
+            sources.append((((x + dx) & 3) * 2 + (h ^ dh), pieces[n * 2 + dh]))
+    for r, source in sources:
+        for i in range(4):
+
+            @pl.when(i < count[r])
+            def _():
+                p = table[r * 4 + i]
+                piece = source[i]
+                out[p] = piece
+                out[F + p] = piece
 
 
 def strip_kernel(fs, pieces, panels, strip, upper, keep, send, tmp, panel, sems):
@@ -191,7 +199,9 @@
     fetch = pltpu.make_async_copy(panels.at[x, 0], panel, sems.at[0])
     fetch.start()
     h, c = lax.axis_index("h"), lax.axis_index("c")
-    parts = [pieces[:, ch].reshape(S, HALF) for ch in range(2)]
+    parts = [
+        jnp.stack([pieces[0, :, ch], pieces[1, :, ch]], axis=1).reshape(S, HALF) for ch in range(2)
+    ]
     value = jnp.concatenate(parts, axis=1)
     strip[...] = -value
     store = pltpu.make_async_copy(strip, upper.at[x, 0], sems.at[1])
@@ -237,6 +247,11 @@
     return lax.all_to_all(value, axes, 0, 0, tiled=True)
 
 
+def row_hop(value, dx, dh):
+    pairs = [(x * 2 + h, (x + dx) % 4 * 2 + (h ^ dh)) for x in range(4) for h in range(2)]
+    return lax.ppermute(value, ROW, pairs)
+
+
 def gather_x(value):
     half = value.shape[0] // 2
     before = hop(value, "x", 1)
@@ -247,7 +262,7 @@
 
 
 def local(ancestor, panels, diag_inverse, fs):
-    x, c = lax.axis_index("x"), lax.axis_index("c")
+    x, h, c = lax.axis_index("x"), lax.axis_index("h"), lax.axis_index("c")
     packed = call(
         pack_kernel, fs, [panels], (8, 2, FRONT, HALF), in_specs=[HBM],
         scratch=[pltpu.VMEM((S, W), jnp.float32), pltpu.SemaphoreType.DMA], mib=60,
@@ -274,31 +289,38 @@
         n = len(steps)
         return call(
             functools.partial(product_kernel, steps, base), fs,
-            [*pair, *blocks, *behind], (16, n, 4, PIECE, HALF),
+            [*pair, *blocks, *behind],
+            (16, n, 4, PIECE, HALF) if steps == (2,) else (8, n, 4, FRONT, HALF),
             in_specs=[HBM] * 2 + [VMEM] * len(blocks) + [ANY] * len(behind),
             scratch=[pltpu.VMEM((n, 2, 2, 4, S, S), jnp.float32),
                      pltpu.SemaphoreType.DMA((n, 2, 2, 4))],
-            flops=n * 10**9, mib=8 * n + 6,
+            flops=n * 10**9, mib=14 if n == 1 and base == 0 else 50,
         )
 
-    def total(value):
-        value = exchange(value, SHEET)
-        value = value.reshape(2, 8, *value.shape[1:])
-        return [value[:, :, n].sum(1) for n in range(value.shape[2])]
+    def halves(value):
+        value = exchange(value, PLANE).sum(0).reshape(-1, 4, 2, PIECE, HALF)
+        return [
+            [lax.dynamic_index_in_dim(part, side, 1, keepdims=False) for side in (h, 1 - h)]
+            for part in value
+        ]
 
     own_product = product((0,), 0, first_pair, [panel])
-    (own,) = total(own_product)
+    ((own, own_send),) = halves(own_product)
     near_product = product((3, 1), 0, rest_pair, [before, after], [own])
-    near = total(near_product)
+    near = halves(near_product)
     far_product = product((2,), 2, rest_pair, [top, bottom], [near_product])
     near, far_product = lax.optimization_barrier((near, far_product))
-    (far,) = total(far_product)
-    sources = [own, hop(near[0], "x", -1), hop(far, "x", 2), hop(near[1], "x", 1)]
+    far = exchange(far_product, SHEET)
+    far = far.reshape(2, 8, 4, PIECE, HALF).sum(1)
+    sources = [row_hop(own_send, 0, 1)]
+    for (keep, send), dx in zip(near, (-1, 1), strict=True):
+        sources += [row_hop(keep, dx, 0), row_hop(send, dx, 1)]
+    sources = [own, jnp.stack(sources), hop(far, "x", 2)]
     homes = call(
         homes_kernel, fs, sources, (2 * F, PIECE, HALF),
         scratch=[pltpu.SMEM((32,), jnp.int32), pltpu.SMEM((8,), jnp.int32)],
     )
-    placed = exchange(homes, ("h", *COL)).reshape(16, 2, PIECE, HALF)
+    placed = exchange(homes, ("h", *COL)).reshape(2, 8, 2, PIECE, HALF)
     strip, upper, part, part_send = call(
         strip_kernel, fs, [placed, panels],
         [(S, W), (K, 1, S, W), (4, 8, 8, HALF), (4, 8, 8, HALF)], in_specs=[VMEM, HBM],

time: 205 us -> 204 us (level)
  local copies, waits for them, and re-layouts: 9.56 us -> 4.07 us
  starting transfers between devices: 41.8 us -> 43.9 us
    ppermute x0 -> x5, waiting for transfers between devices: none -> 12.9 us  [row_hop(): return lax.ppermute(value, ROW, pairs)]
    ppermute x0 -> x5, starting transfers between devices: none -> 8.9 us  [row_hop(): return lax.ppermute(value, ROW, pairs)]
    ppermute x15 -> x13, waiting for transfers between devices: 24.7 us -> 18.3 us  [hop(): lax.ppermute(value, axis, [(i, (i + shift) % size) for i in range(size)])]
    unnamed x14, local copies, waits for them, and re-layouts: 5.6 us -> 0.05 us
    all_to_all x5, waiting for transfers between devices: 40.4 us -> 35.3 us  [exchange(): return lax.all_to_all(value, axes, 0, 0, tiled=True)]
    ppermute x15 -> x13, starting transfers between devices: 18.9 us -> 14.2 us  [hop(): lax.ppermute(value, axis, [(i, (i + shift) % size) for i in range(size)])]
    all_to_all x5, starting transfers between devices: 22.8 us -> 20.8 us  [exchange(): return lax.all_to_all(value, axes, 0, 0, tiled=True)]
  transfers between devices with their start and end apart: 20 -> 23, of which waited for: 9 -> 12; matrix products, arithmetic and copies ran while one was open for 4% -> 4% of each run, Pallas kernels for 3% -> 3%
where the time goes in v2:
time: 204 us; the launch traced here: 203 us
  waiting for transfers between devices  66.4 us (33%)
  blocking collectives  55.6 us (27%)
  starting transfers between devices  43.9 us (22%)
  Pallas kernels  25.5 us (12%)
  other arithmetic  6.05 us (3%)
  local copies, waits for them, and re-layouts  4.07 us (2%)
    all_to_all x3, blocking collectives, exchange(): return lax.all_to_all(value, axes, 0, 0, tiled=True)  55.6 us
    all_to_all x5, waiting for transfers between devices, exchange(): return lax.all_to_all(value, axes, 0, 0, tiled=True)  35.3 us
    pallas_call x8, Pallas kernels, call(): pl.pallas_call(kernel, out_shape=out_shape[0] if single else out_shape, i...  25.5 us
    all_to_all x5, starting transfers between devices, exchange(): return lax.all_to_all(value, axes, 0, 0, tiled=True)  20.8 us
    ppermute x13, waiting for transfers between devices, hop(): lax.ppermute(value, axis, [(i, (i + shift) % size) for i in range(size)])  18.3 us
    ppermute x13, starting transfers between devices, hop(): lax.ppermute(value, axis, [(i, (i + shift) % size) for i in range(size)])  14.2 us
    ppermute x5, waiting for transfers between devices, row_hop(): return lax.ppermute(value, ROW, pairs)  12.9 us
    ppermute x5, starting transfers between devices, row_hop(): return lax.ppermute(value, ROW, pairs)  8.9 us
  transfers between devices with their start and end apart: 23, of which 12 were waited for; matrix products, arithmetic and copies ran while one was open for 4% of the time, Pallas kernels for 3%

profile of v2, /device:TPU:1, one launch (start us, length us, event | category | flops | bytes accessed | tf_op | source)
XLA Modules:
  0.0 202.5 jit_solution(14547098390402552391)
XLA Ops:
  0.6 2.6 %shard_map.59.after = f32[8,2,32,256]{3,2,1,0:T(8,128)} custom-call(s32[4,16]{1,0:T(4,128)} %fs.15, f32[4,1,256,512]{3,2,1,0:T(8,128)} %panels.3), custom_call_target="tpu_custom_call" | custom-call | bytes 1048576 | tf_op jit(solution)/shard_map/pallas_call | solution.py:230
  3.2 4.6 %shard_map.60 = (f32[1,2,4,256,256]{4,3,2,1,0:T(8,128)}, f32[3,2,4,256,256]{4,3,2,1,0:T(8,128)}) custom-call(s32[4,16]{1,0:T(4,128)} %fs.15, f32[3072,1536]{1,0:T(8,128)} %ancestor.1, f32[8,2,32,256]{3,2,1,0:T(8,128)} %shard_map.59.after), custom_call_target="tpu_custom_call" | custom-call | bytes 16777216 | tf_op jit(solution)/shard_map/pallas_call | solution.py:230
  7.8 1.2 collective-permute-start.2
  9.1 16.2 %all_to_all.40.pieces = f32[16,32,256]{2,1,0:T(8,128)S(1)} all-to-all(f32[16,32,256]{2,1,0:T(8,128)S(1)} %bitcast.49), channel_id=1, replica_groups=mesh['x'=4,'h'=2,'l'=2,'z'=4,'c'=2] {'l','z','c'}, dimensions={0} | all-to-all | bytes 1048576 | tf_op jit(solution)/shard_map/all_to_all | solution.py:247
  25.2 0.7 shard_map.61
  26.0 17.5 %all_to_all.41.refs_0_ = f32[8,4,32,256]{3,2,1,0:T(8,128)S(1)} all-to-all(f32[8,4,32,256]{3,2,1,0:T(8,128)S(1)} %bitcast.47), channel_id=1, replica_groups=mesh['x'=4,'h'=2,'l'=2,'z'=4,'c'=2] {'l','z'}, dimensions={0} | all-to-all | bytes 2097152 | tf_op jit(solution)/shard_map/all_to_all | solution.py:247
  43.5 2.4 %collective-permute-start.4 = (f32[8,4,32,256]{3,2,1,0:T(8,128)S(1)}, f32[8,4,32,256]{3,2,1,0:T(8,128)S(1)}, u32[]{:S(2)}, u32[]{:S(2)}) collective-permute-start(f32[8,4,32,256]{3,2,1,0:T(8,128)S(1)} %all_to_all.41.refs_0_), channel_id=1, source_target_pairs={{0,96},{32,0},{64,32},{96,64},{1,97},{33,1},{65,33},{97,65},{2,98}... | collective-permute-start | bytes 3145736 | tf_op jit(solution)/shard_map/ppermute | solution.py:243
  45.8 2.2 %shard_map.62 = f32[8,1,4,32,256]{4,3,2,1,0:T(8,128)} custom-call(s32[4,16]{1,0:T(4,128)S(1)} %copy-done.2, f32[1,2,4,256,256]{4,3,2,1,0:T(8,128)S(1)} %copy-done.1, f32[1,2,4,256,256]{4,3,2,1,0:T(8,128)S(1)} %collective-permute-done.theirs, f32[8,4,32,256]{3,2,1,0:T(8,128)S(1)} %all_to_all.41.refs_0_), custom_call_target="tpu_custom_call" | custom-call | flops 1000000000 | bytes 2097152 | tf_op jit(solution)/shard_map/pallas_call | solution.py:230
  48.1 4.3 %all-to-all-start.2 = ((f32[8,1,4,32,256]{4,3,2,1,0:T(8,128)}), f32[8,1,4,32,256]{4,3,2,1,0:T(8,128)}, u32[]{:S(2)}, u32[]{:S(2)}) async-start(f32[8,1,4,32,256]{4,3,2,1,0:T(8,128)} %shard_map.62), calls=%async_computation.2 | async-start | bytes 2097152 | tf_op jit(solution)/shard_map/all_to_all | solution.py:247
  52.4 11.4 %all-to-all-done.2 = f32[8,1,4,32,256]{4,3,2,1,0:T(8,128)} async-done(((f32[8,1,4,32,256]{4,3,2,1,0:T(8,128)}), f32[8,1,4,32,256]{4,3,2,1,0:T(8,128)}, u32[]{:S(2)}, u32[]{:S(2)}) %all-to-all-start.2) | async-done | bytes 1048608 | tf_op jit(solution)/shard_map/all_to_all | solution.py:247
  63.8 1.3 reduce_sum.36
  65.1 1.1 collective-permute-done.4.refs_1_
  66.2 3.1 %collective-permute-done.3.refs_0_ = f32[8,4,32,256]{3,2,1,0:T(8,128)S(1)} collective-permute-done((f32[8,4,32,256]{3,2,1,0:T(8,128)S(1)}, f32[8,4,32,256]{3,2,1,0:T(8,128)S(1)}, u32[]{:S(2)}, u32[]{:S(2)}) %collective-permute-start.3) | collective-permute-done | bytes 1048608 | tf_op jit(solution)/shard_map/ppermute | solution.py:243
  69.3 9.0 %shard_map.63.refs_2_ = f32[8,2,4,32,256]{4,3,2,1,0:T(8,128)} custom-call(s32[4,16]{1,0:T(4,128)S(1)} %copy-done.2, f32[3,2,4,256,256]{4,3,2,1,0:T(8,128)} %get-tuple-element.14.mine, f32[3,2,4,256,256]{4,3,2,1,0:T(8,128)} %collective-permute-done.2.theirs, f32[8,4,32,256]{3,2,1,0:T(8,128)S(1)} %collective-permute-done.3.refs_0_, ...), custom_call_target="tpu_custom_call" | custom-call | flops 2000000000 | bytes 4194304 | tf_op jit(solution)/shard_map/pallas_call | solution.py:230
  78.3 4.4 %all-to-all-start.3 = ((f32[8,2,4,32,256]{4,3,2,1,0:T(8,128)}), f32[8,2,4,32,256]{4,3,2,1,0:T(8,128)}, u32[]{:S(2)}, u32[]{:S(2)}) async-start(f32[8,2,4,32,256]{4,3,2,1,0:T(8,128)} %shard_map.63.refs_2_), calls=%async_computation.3 | async-start | bytes 4194304 | tf_op jit(solution)/shard_map/all_to_all | solution.py:247
  82.8 1.5 collective-permute-start.5
  84.4 8.7 %collective-permute-done.6.refs_1_ = f32[4,4,32,256]{3,2,1,0:T(8,128)S(1)} collective-permute-done((f32[4,4,32,256]{3,2,1,0:T(8,128)S(1)}, f32[4,4,32,256]{3,2,1,0:T(8,128)S(1)}, u32[]{:S(2)}, u32[]{:S(2)}) %collective-permute-start.6) | collective-permute-done | bytes 524320 | tf_op jit(solution)/shard_map/ppermute | solution.py:243
  93.1 1.3 collective-permute-done.5.refs_0_
  94.4 3.9 %shard_map.64 = f32[16,1,4,16,256]{4,3,2,1,0:T(8,128)} custom-call(s32[4,16]{1,0:T(4,128)S(1)} %copy-done.2, f32[3,2,4,256,256]{4,3,2,1,0:T(8,128)} %get-tuple-element.14.mine, f32[3,2,4,256,256]{4,3,2,1,0:T(8,128)} %collective-permute-done.2.theirs, f32[4,4,32,256]{3,2,1,0:T(8,128)S(1)} %collective-permute-done.5.refs_0_, ...), custom_call_target="tpu_custom_call" | custom-call | flops 1000000000 | bytes 2097152 | tf_op jit(solution)/shard_map/pallas_call | solution.py:230
  98.3 10.0 %all-to-all-done.3 = f32[8,2,4,32,256]{4,3,2,1,0:T(8,128)} async-done(((f32[8,2,4,32,256]{4,3,2,1,0:T(8,128)}), f32[8,2,4,32,256]{4,3,2,1,0:T(8,128)}, u32[]{:S(2)}, u32[]{:S(2)}) %all-to-all-start.3) | async-done | bytes 2097184 | tf_op jit(solution)/shard_map/all_to_all | solution.py:247
  108.3 1.8 reduce_sum.37
  110.1 4.4 %all-to-all-start.4 = ((f32[16,1,4,16,256]{4,3,2,1,0:T(8,128)}), f32[16,1,4,16,256]{4,3,2,1,0:T(8,128)}, u32[]{:S(2)}, u32[]{:S(2)}) async-start(f32[16,1,4,16,256]{4,3,2,1,0:T(8,128)} %shard_map.64), calls=%async_computation.4 | async-start | bytes 2097152 | tf_op jit(solution)/shard_map/all_to_all | solution.py:247
  114.5 2.9 %collective-permute-start.1 = (f32[4,16,256]{2,1,0:T(8,128)S(1)}, f32[4,16,256]{2,1,0:T(8,128)S(1)}, u32[]{:S(2)}, u32[]{:S(2)}) collective-permute-start(f32[4,16,256]{2,1,0:T(8,128)S(1)} %get-tuple-element.30), channel_id=1, source_target_pairs={{0,16},{16,0},{32,48},{48,32},{64,80},{80,64},{96,112},{112,96},{1... | collective-permute-start | bytes 196616 | tf_op jit(solution)/shard_map/ppermute | solution.py:252
  117.4 2.1 %collective-permute-start.7 = (f32[4,16,256]{2,1,0:T(8,128)S(1)}, f32[4,16,256]{2,1,0:T(8,128)S(1)}, u32[]{:S(2)}, u32[]{:S(2)}) collective-permute-start(f32[4,16,256]{2,1,0:T(8,128)S(1)} %get-tuple-element.15), channel_id=1, source_target_pairs={{0,96},{16,112},{32,0},{48,16},{64,32},{80,48},{96,64},{112,80},{1... | collective-permute-start | bytes 196616 | tf_op jit(solution)/shard_map/ppermute | solution.py:252
  119.6 10.2 %collective-permute-done.1 = f32[4,16,256]{2,1,0:T(8,128)S(1)} collective-permute-done((f32[4,16,256]{2,1,0:T(8,128)S(1)}, f32[4,16,256]{2,1,0:T(8,128)S(1)}, u32[]{:S(2)}, u32[]{:S(2)}) %collective-permute-start.1) | collective-permute-done | bytes 65568 | tf_op jit(solution)/shard_map/ppermute | solution.py:252
  129.8 2.2 %collective-permute-start.8 = (f32[4,16,256]{2,1,0:T(8,128)S(1)}, f32[4,16,256]{2,1,0:T(8,128)S(1)}, u32[]{:S(2)}, u32[]{:S(2)}) collective-permute-start(f32[4,16,256]{2,1,0:T(8,128)S(1)} %get-tuple-element.16), channel_id=1, source_target_pairs={{0,112},{16,96},{32,16},{48,0},{64,48},{80,32},{96,80},{112,64},{1... | collective-permute-start | bytes 196616 | tf_op jit(solution)/shard_map/ppermute | solution.py:252
  132.0 1.6 collective-permute-start.10
  133.7 1.6 collective-permute-done.8
  135.3 1.0 collective-permute-done.9
  136.4 1.3 bitcast_reduce_fusion
  137.7 2.3 %collective-permute-start.11 = (f32[2,4,16,256]{3,2,1,0:T(8,128)S(1)}, f32[2,4,16,256]{3,2,1,0:T(8,128)S(1)}, u32[]{:S(2)}, u32[]{:S(2)}) collective-permute-start(f32[2,4,16,256]{3,2,1,0:T(8,128)S(1)} %bitcast_reduce_fusion), channel_id=1, source_target_pairs={{0,64},{32,96},{64,0},{96,32},{1,65},{33,97},{65,1},{97,33},{2,66}... | collective-permute-start | bytes 393224 | tf_op jit(solution)/shard_map/ppermute | solution.py:243
  140.0 4.0 %collective-permute-done.11.refs_2_ = f32[2,4,16,256]{3,2,1,0:T(8,128)S(1)} collective-permute-done((f32[2,4,16,256]{3,2,1,0:T(8,128)S(1)}, f32[2,4,16,256]{3,2,1,0:T(8,128)S(1)}, u32[]{:S(2)}, u32[]{:S(2)}) %collective-permute-start.11) | collective-permute-done | bytes 131104 | tf_op jit(solution)/shard_map/ppermute | solution.py:243
  144.0 1.0 shard_map.65
  145.0 22.0 %all_to_all.42 = f32[32,16,256]{2,1,0:T(8,128)S(1)} all-to-all(f32[32,16,256]{2,1,0:T(8,128)S(1)} %shard_map.65), channel_id=1, replica_groups=mesh['x'=4,'h'=2,'l'=2,'z'=4,'c'=2] {'h','l','z','c'}, dimensions={0} | all-to-all | bytes 1048576 | tf_op jit(solution)/shard_map/all_to_all | solution.py:247
  167.0 1.5 shard_map.66
  169.1 1.0 collective-permute-start.12
  170.1 0.7 add.46
  170.9 4.3 %all-to-all-start.6 = ((f32[32,8,256]{2,1,0:T(8,128)}), f32[32,8,256]{2,1,0:T(8,128)S(1)}, u32[]{:S(2)}, u32[]{:S(2)}) async-start(f32[32,8,256]{2,1,0:T(8,128)} %bitcast.22), calls=%async_computation.6 | async-start | bytes 524288 | tf_op jit(solution)/shard_map/all_to_all | solution.py:247
  175.2 11.2 %all-to-all-done.6 = f32[32,8,256]{2,1,0:T(8,128)S(1)} async-done(((f32[32,8,256]{2,1,0:T(8,128)}), f32[32,8,256]{2,1,0:T(8,128)S(1)}, u32[]{:S(2)}, u32[]{:S(2)}) %all-to-all-start.6) | async-done | bytes 262176 | tf_op jit(solution)/shard_map/all_to_all | solution.py:247
  186.5 0.7 broadcast_in_dim.22
  187.2 3.4 %all-to-all-start.7 = ((f32[8,4,8,256]{3,2,1,0:T(8,128)}), f32[8,4,8,256]{3,2,1,0:T(8,128)S(1)}, u32[]{:S(2)}, u32[]{:S(2)}) async-start(f32[8,4,8,256]{3,2,1,0:T(8,128)} %broadcast_in_dim.22), calls=%async_computation.7 | async-start | bytes 524288 | tf_op jit(solution)/shard_map/all_to_all | solution.py:247
  190.7 0.8 collective-permute-start.15
  191.5 0.8 collective-permute-start.14
  192.3 0.8 bitcast_dynamic-update-slice_fusion.1
  193.1 0.8 bitcast_dynamic-update-slice_fusion
  194.0 2.7 %all-to-all-done.7 = f32[8,4,8,256]{3,2,1,0:T(8,128)S(1)} async-done(((f32[8,4,8,256]{3,2,1,0:T(8,128)}), f32[8,4,8,256]{3,2,1,0:T(8,128)S(1)}, u32[]{:S(2)}, u32[]{:S(2)}) %all-to-all-start.7) | async-done | bytes 262176 | tf_op jit(solution)/shard_map/all_to_all | solution.py:247
  196.7 3.5 %collective-permute-start.17 = (f32[4,64,256]{2,1,0:T(8,128)S(1)}, f32[4,64,256]{2,1,0:T(8,128)S(1)}, u32[]{:S(2)}, u32[]{:S(2)}) collective-permute-start(f32[4,64,256]{2,1,0:T(8,128)S(1)} %bitcast.50), channel_id=1, source_target_pairs={{0,1},{1,0},{2,3},{3,2},{4,5},{5,4},{6,7},{7,6},{8,9},{9,8},{10,11... | collective-permute-start | bytes 786440 | tf_op jit(solution)/shard_map/ppermute | solution.py:243
  201.6 0.9 fusion
  (43 shorter events, 2.5 us)
Async XLA Ops:
  3.2 5.9 %copy-start.3 = (f32[8,2,32,256]{3,2,1,0:T(8,128)S(1)}, f32[8,2,32,256]{3,2,1,0:T(8,128)}, u32[]{:S(2)}) copy-start(f32[8,2,32,256]{3,2,1,0:T(8,128)} %shard_map.59.after) | copy-start | bytes 1572868
  3.2 22.0 %copy-start.2 = (s32[4,16]{1,0:T(4,128)S(1)}, s32[4,16]{1,0:T(4,128)}, u32[]{:S(2)}) copy-start(s32[4,16]{1,0:T(4,128)} %fs.15) | copy-start | bytes 772
  7.8 61.5 %collective-permute-start.2 = (f32[3,2,4,256,256]{4,3,2,1,0:T(8,128)}, f32[3,2,4,256,256]{4,3,2,1,0:T(8,128)}, u32[]{:S(2)}, u32[]{:S(2)}) collective-permute-start(f32[3,2,4,256,256]{4,3,2,1,0:T(8,128)} %get-tuple-element.14.mine), channel_id=1, source_target_pairs={{0,1},{1,0},{2,3},{3,2},{4,5},{5,4},{6,7},{7,6},{8,9},{9,8},{10,11... | collective-permute-start | bytes 18874376 | tf_op jit(solution)/shard_map/ppermute | solution.py:243
  9.0 36.9 %collective-permute-start = (f32[1,2,4,256,256]{4,3,2,1,0:T(8,128)}, f32[1,2,4,256,256]{4,3,2,1,0:T(8,128)S(1)}, u32[]{:S(2)}, u32[]{:S(2)}) collective-permute-start(f32[1,2,4,256,256]{4,3,2,1,0:T(8,128)} %get-tuple-element.13.mine), channel_id=1, source_target_pairs={{0,1},{1,0},{2,3},{3,2},{4,5},{5,4},{6,7},{7,6},{8,9},{9,8},{10,11... | collective-permute-start | bytes 6291464 | tf_op jit(solution)/shard_map/ppermute | solution.py:243
  25.2 20.6 %copy-start.1 = (f32[1,2,4,256,256]{4,3,2,1,0:T(8,128)S(1)}, f32[1,2,4,256,256]{4,3,2,1,0:T(8,128)}, u32[]{:S(2)}) copy-start(f32[1,2,4,256,256]{4,3,2,1,0:T(8,128)} %get-tuple-element.13.mine) | copy-start | bytes 6291460
  43.5 22.7 %collective-permute-start.4 = (f32[8,4,32,256]{3,2,1,0:T(8,128)S(1)}, f32[8,4,32,256]{3,2,1,0:T(8,128)S(1)}, u32[]{:S(2)}, u32[]{:S(2)}) collective-permute-start(f32[8,4,32,256]{3,2,1,0:T(8,128)S(1)} %all_to_all.41.refs_0_), channel_id=1, source_target_pairs={{0,96},{32,0},{64,32},{96,64},{1,97},{33,1},{65,33},{97,65},{2,98}... | collective-permute-start | bytes 3145736 | tf_op jit(solution)/shard_map/ppermute | solution.py:243
  45.8 23.5 %collective-permute-start.3 = (f32[8,4,32,256]{3,2,1,0:T(8,128)S(1)}, f32[8,4,32,256]{3,2,1,0:T(8,128)S(1)}, u32[]{:S(2)}, u32[]{:S(2)}) collective-permute-start(f32[8,4,32,256]{3,2,1,0:T(8,128)S(1)} %all_to_all.41.refs_0_), channel_id=1, source_target_pairs={{0,32},{32,64},{64,96},{96,0},{1,33},{33,65},{65,97},{97,1},{2,34}... | collective-permute-start | bytes 3145736 | tf_op jit(solution)/shard_map/ppermute | solution.py:243
  48.1 15.7 %all-to-all-start.2 = ((f32[8,1,4,32,256]{4,3,2,1,0:T(8,128)}), f32[8,1,4,32,256]{4,3,2,1,0:T(8,128)}, u32[]{:S(2)}, u32[]{:S(2)}) async-start(f32[8,1,4,32,256]{4,3,2,1,0:T(8,128)} %shard_map.62), calls=%async_computation.2 | async-start | bytes 2097152 | tf_op jit(solution)/shard_map/all_to_all | solution.py:247
  78.3 30.0 %all-to-all-start.3 = ((f32[8,2,4,32,256]{4,3,2,1,0:T(8,128)}), f32[8,2,4,32,256]{4,3,2,1,0:T(8,128)}, u32[]{:S(2)}, u32[]{:S(2)}) async-start(f32[8,2,4,32,256]{4,3,2,1,0:T(8,128)} %shard_map.63.refs_2_), calls=%async_computation.3 | async-start | bytes 4194304 | tf_op jit(solution)/shard_map/all_to_all | solution.py:247
  82.7 10.3 %collective-permute-start.6 = (f32[4,4,32,256]{3,2,1,0:T(8,128)S(1)}, f32[4,4,32,256]{3,2,1,0:T(8,128)S(1)}, u32[]{:S(2)}, u32[]{:S(2)}) collective-permute-start(f32[4,4,32,256]{3,2,1,0:T(8,128)S(1)} %slice.19), channel_id=1, source_target_pairs={{0,96},{32,0},{64,32},{96,64},{1,97},{33,1},{65,33},{97,65},{2,98}... | collective-permute-start | bytes 1572872 | tf_op jit(solution)/shard_map/ppermute | solution.py:243
  82.8 11.6 %collective-permute-start.5 = (f32[4,4,32,256]{3,2,1,0:T(8,128)S(1)}, f32[4,4,32,256]{3,2,1,0:T(8,128)S(1)}, u32[]{:S(2)}, u32[]{:S(2)}) collective-permute-start(f32[4,4,32,256]{3,2,1,0:T(8,128)S(1)} %slice.18), channel_id=1, source_target_pairs={{0,32},{32,64},{64,96},{96,0},{1,33},{33,65},{65,97},{97,1},{2,34}... | collective-permute-start | bytes 1572872 | tf_op jit(solution)/shard_map/ppermute | solution.py:243
  110.1 26.3 %all-to-all-start.4 = ((f32[16,1,4,16,256]{4,3,2,1,0:T(8,128)}), f32[16,1,4,16,256]{4,3,2,1,0:T(8,128)}, u32[]{:S(2)}, u32[]{:S(2)}) async-start(f32[16,1,4,16,256]{4,3,2,1,0:T(8,128)} %shard_map.64), calls=%async_computation.4 | async-start | bytes 2097152 | tf_op jit(solution)/shard_map/all_to_all | solution.py:247
  114.5 52.5 %copy-start = (f32[4,1,256,512]{3,2,1,0:T(8,128)S(1)}, f32[4,1,256,512]{3,2,1,0:T(8,128)}, u32[]{:S(2)}) copy-start(f32[4,1,256,512]{3,2,1,0:T(8,128)} %panels.3) | copy-start | bytes 6291460
  114.5 15.3 %collective-permute-start.1 = (f32[4,16,256]{2,1,0:T(8,128)S(1)}, f32[4,16,256]{2,1,0:T(8,128)S(1)}, u32[]{:S(2)}, u32[]{:S(2)}) collective-permute-start(f32[4,16,256]{2,1,0:T(8,128)S(1)} %get-tuple-element.30), channel_id=1, source_target_pairs={{0,16},{16,0},{32,48},{48,32},{64,80},{80,64},{96,112},{112,96},{1... | collective-permute-start | bytes 196616 | tf_op jit(solution)/shard_map/ppermute | solution.py:252
  117.4 16.3 %collective-permute-start.7 = (f32[4,16,256]{2,1,0:T(8,128)S(1)}, f32[4,16,256]{2,1,0:T(8,128)S(1)}, u32[]{:S(2)}, u32[]{:S(2)}) collective-permute-start(f32[4,16,256]{2,1,0:T(8,128)S(1)} %get-tuple-element.15), channel_id=1, source_target_pairs={{0,96},{16,112},{32,0},{48,16},{64,32},{80,48},{96,64},{112,80},{1... | collective-permute-start | bytes 196616 | tf_op jit(solution)/shard_map/ppermute | solution.py:252
  129.8 5.5 %collective-permute-start.8 = (f32[4,16,256]{2,1,0:T(8,128)S(1)}, f32[4,16,256]{2,1,0:T(8,128)S(1)}, u32[]{:S(2)}, u32[]{:S(2)}) collective-permute-start(f32[4,16,256]{2,1,0:T(8,128)S(1)} %get-tuple-element.16), channel_id=1, source_target_pairs={{0,112},{16,96},{32,16},{48,0},{64,48},{80,32},{96,80},{112,64},{1... | collective-permute-start | bytes 196616 | tf_op jit(solution)/shard_map/ppermute | solution.py:252
  132.0 4.3 %collective-permute-start.9 = (f32[4,16,256]{2,1,0:T(8,128)S(1)}, f32[4,16,256]{2,1,0:T(8,128)S(1)}, u32[]{:S(2)}, u32[]{:S(2)}) collective-permute-start(f32[4,16,256]{2,1,0:T(8,128)S(1)} %get-tuple-element.17), channel_id=1, source_target_pairs={{0,32},{16,48},{32,64},{48,80},{64,96},{80,112},{96,0},{112,16},{1... | collective-permute-start | bytes 196616 | tf_op jit(solution)/shard_map/ppermute | solution.py:252
  132.0 7.9 %collective-permute-start.10 = (f32[4,16,256]{2,1,0:T(8,128)S(1)}, f32[4,16,256]{2,1,0:T(8,128)S(1)}, u32[]{:S(2)}, u32[]{:S(2)}) collective-permute-start(f32[4,16,256]{2,1,0:T(8,128)S(1)} %get-tuple-element.18), channel_id=1, source_target_pairs={{0,48},{16,32},{32,80},{48,64},{64,112},{80,96},{96,16},{112,0},{1... | collective-permute-start | bytes 196616 | tf_op jit(solution)/shard_map/ppermute | solution.py:252
  137.7 6.3 %collective-permute-start.11 = (f32[2,4,16,256]{3,2,1,0:T(8,128)S(1)}, f32[2,4,16,256]{3,2,1,0:T(8,128)S(1)}, u32[]{:S(2)}, u32[]{:S(2)}) collective-permute-start(f32[2,4,16,256]{3,2,1,0:T(8,128)S(1)} %bitcast_reduce_fusion), channel_id=1, source_target_pairs={{0,64},{32,96},{64,0},{96,32},{1,65},{33,97},{65,1},{97,33},{2,66}... | collective-permute-start | bytes 393224 | tf_op jit(solution)/shard_map/ppermute | solution.py:243
  168.5 1.6 collective-permute-start.16
  168.6 22.0 %collective-permute-start.13 = (f32[256,512]{1,0:T(8,128)S(1)}, f32[256,512]{1,0:T(8,128)S(1)}, u32[]{:S(2)}, u32[]{:S(2)}) collective-permute-start(f32[256,512]{1,0:T(8,128)S(1)} %get-tuple-element.21), channel_id=1, source_target_pairs={{0,96},{32,0},{64,32},{96,64},{1,97},{33,1},{65,33},{97,65},{2,98}... | collective-permute-start | bytes 1572872 | tf_op jit(solution)/shard_map/ppermute | solution.py:243
  169.1 22.3 %collective-permute-start.12 = (f32[256,512]{1,0:T(8,128)S(1)}, f32[256,512]{1,0:T(8,128)S(1)}, u32[]{:S(2)}, u32[]{:S(2)}) collective-permute-start(f32[256,512]{1,0:T(8,128)S(1)} %get-tuple-element.21), channel_id=1, source_target_pairs={{0,32},{32,64},{64,96},{96,0},{1,33},{33,65},{65,97},{97,1},{2,34}... | collective-permute-start | bytes 1572872 | tf_op jit(solution)/shard_map/ppermute | solution.py:243
  170.9 15.6 %all-to-all-start.6 = ((f32[32,8,256]{2,1,0:T(8,128)}), f32[32,8,256]{2,1,0:T(8,128)S(1)}, u32[]{:S(2)}, u32[]{:S(2)}) async-start(f32[32,8,256]{2,1,0:T(8,128)} %bitcast.22), calls=%async_computation.6 | async-start | bytes 524288 | tf_op jit(solution)/shard_map/all_to_all | solution.py:247
  187.2 9.4 %all-to-all-start.7 = ((f32[8,4,8,256]{3,2,1,0:T(8,128)}), f32[8,4,8,256]{3,2,1,0:T(8,128)S(1)}, u32[]{:S(2)}, u32[]{:S(2)}) async-start(f32[8,4,8,256]{3,2,1,0:T(8,128)} %broadcast_in_dim.22), calls=%async_computation.7 | async-start | bytes 524288 | tf_op jit(solution)/shard_map/all_to_all | solution.py:247
  190.7 11.0 %copy-start.4 = (f32[4,64,512]{2,1,0:T(8,128)S(1)}, f32[4,64,512]{2,1,0:T(8,128)}, u32[]{:S(2)}) copy-start(f32[4,64,512]{2,1,0:T(8,128)} %param.6) | copy-start | bytes 1572868
  190.7 10.2 %collective-permute-start.15 = (f32[128,512]{1,0:T(8,128)S(1)}, f32[128,512]{1,0:T(8,128)S(1)}, u32[]{:S(2)}, u32[]{:S(2)}) collective-permute-start(f32[128,512]{1,0:T(8,128)S(1)} %slice.21), channel_id=1, source_target_pairs={{0,96},{32,0},{64,32},{96,64},{1,97},{33,1},{65,33},{97,65},{2,98}... | collective-permute-start | bytes 786440 | tf_op jit(solution)/shard_map/ppermute | solution.py:243
  191.5 8.7 %collective-permute-start.14 = (f32[128,512]{1,0:T(8,128)S(1)}, f32[128,512]{1,0:T(8,128)S(1)}, u32[]{:S(2)}, u32[]{:S(2)}) collective-permute-start(f32[128,512]{1,0:T(8,128)S(1)} %slice.20), channel_id=1, source_target_pairs={{0,32},{32,64},{64,96},{96,0},{1,33},{33,65},{65,97},{97,1},{2,34}... | collective-permute-start | bytes 786440 | tf_op jit(solution)/shard_map/ppermute | solution.py:243
  196.7 5.0 %collective-permute-start.17 = (f32[4,64,256]{2,1,0:T(8,128)S(1)}, f32[4,64,256]{2,1,0:T(8,128)S(1)}, u32[]{:S(2)}, u32[]{:S(2)}) collective-permute-start(f32[4,64,256]{2,1,0:T(8,128)S(1)} %bitcast.50), channel_id=1, source_target_pairs={{0,1},{1,0},{2,3},{3,2},{4,5},{5,4},{6,7},{7,6},{8,9},{9,8},{10,11... | collective-permute-start | bytes 786440 | tf_op jit(solution)/shard_map/ppermute | solution.py:243

commit v3 on v1

--- a/solution.py
+++ b/solution.py
@@ -278,7 +278,7 @@
             in_specs=[HBM] * 2 + [VMEM] * len(blocks) + [ANY] * len(behind),
             scratch=[pltpu.VMEM((n, 2, 2, 4, S, S), jnp.float32),
                      pltpu.SemaphoreType.DMA((n, 2, 2, 4))],
-            flops=n * 10**9, mib=8 * n + 6,
+            flops=n * 10**9, mib=14 if n == 1 and base == 0 else 50,
         )
 
     def total(value):
@@ -307,7 +307,8 @@
                  pltpu.SemaphoreType.DMA((2,))],
     )
     before, after, top, bottom = gather_x(strip)
-    part = (part + hop(part_send, "c", 1)).reshape(32, 8, HALF)
+    part_other = hop(part_send, "c", 1)
+    part = (part + part_other).reshape(32, 8, HALF)
     part = exchange(part, ("x", *PLANE))
     part = part.reshape(4, 8, 8, HALF).sum(1)
     part = exchange(jnp.broadcast_to(part[None], (8, *part.shape)), PLANE)

time: 205 us -> 202 us (0.985)
  local copies, waits for them, and re-layouts: 9.56 us -> 3.98 us
  waiting for transfers between devices: 65.1 us -> 67.4 us
    unnamed x14 -> x10, local copies, waits for them, and re-layouts: 5.6 us -> 0.03 us
    all_to_all x5, waiting for transfers between devices: 40.4 us -> 42.7 us  [exchange(): return lax.all_to_all(value, axes, 0, 0, tiled=True)]
where the time goes in v3:
time: 202 us; the launch traced here: 201 us
  waiting for transfers between devices  67.4 us (33%)
  blocking collectives  55.9 us (28%)
  starting transfers between devices  41.8 us (21%)
  Pallas kernels  25.4 us (13%)
  other arithmetic  6.06 us (3%)
  local copies, waits for them, and re-layouts  3.98 us (2%)
    all_to_all x3, blocking collectives, exchange(): return lax.all_to_all(value, axes, 0, 0, tiled=True)  55.9 us
    all_to_all x5, waiting for transfers between devices, exchange(): return lax.all_to_all(value, axes, 0, 0, tiled=True)  42.7 us
    pallas_call x8, Pallas kernels, call(): pl.pallas_call(kernel, out_shape=out_shape[0] if single else out_shape, i...  25.4 us
    ppermute x15, waiting for transfers between devices, hop(): lax.ppermute(value, axis, [(i, (i + shift) % size) for i in range(size)])  24.7 us
    all_to_all x5, starting transfers between devices, exchange(): return lax.all_to_all(value, axes, 0, 0, tiled=True)  22.8 us
    ppermute x15, starting transfers between devices, hop(): lax.ppermute(value, axis, [(i, (i + shift) % size) for i in range(size)])  19 us
    reduce_sum x3, other arithmetic, total(): return [value[:, :, n].sum(1) for n in range(value.shape[2])]  4.4 us
  transfers between devices with their start and end apart: 20, of which 9 were waited for; matrix products, arithmetic and copies ran while one was open for 4% of the time, Pallas kernels for 3%

profile of v3, /device:TPU:1, one launch (start us, length us, event | category | flops | bytes accessed | tf_op | source)
XLA Modules:
  0.0 201.4 jit_solution(11047477163522419528)
XLA Ops:
  0.6 2.6 %shard_map.59.after = f32[8,2,32,256]{3,2,1,0:T(8,128)} custom-call(s32[4,16]{1,0:T(4,128)} %fs.15, f32[4,1,256,512]{3,2,1,0:T(8,128)} %panels.3), custom_call_target="tpu_custom_call" | custom-call | bytes 1048576 | tf_op jit(solution)/shard_map/pallas_call | solution.py:220
  3.2 4.6 %shard_map.60 = (f32[1,2,4,256,256]{4,3,2,1,0:T(8,128)}, f32[3,2,4,256,256]{4,3,2,1,0:T(8,128)}) custom-call(s32[4,16]{1,0:T(4,128)} %fs.15, f32[3072,1536]{1,0:T(8,128)} %ancestor.1, f32[8,2,32,256]{3,2,1,0:T(8,128)} %shard_map.59.after), custom_call_target="tpu_custom_call" | custom-call | bytes 16777216 | tf_op jit(solution)/shard_map/pallas_call | solution.py:220
  7.8 1.2 collective-permute-start.1
  9.0 0.1 collective-permute-start
  9.1 16.1 %all_to_all.40.pieces = f32[16,32,256]{2,1,0:T(8,128)S(1)} all-to-all(f32[16,32,256]{2,1,0:T(8,128)S(1)} %bitcast.28), channel_id=1, replica_groups=mesh['x'=4,'h'=2,'l'=2,'z'=4,'c'=2] {'l','z','c'}, dimensions={0} | all-to-all | bytes 1048576 | tf_op jit(solution)/shard_map/all_to_all | solution.py:237
  25.2 0.7 shard_map.61
  26.0 17.5 %all_to_all.41.refs_0_ = f32[8,4,32,256]{3,2,1,0:T(8,128)S(1)} all-to-all(f32[8,4,32,256]{3,2,1,0:T(8,128)S(1)} %bitcast.26), channel_id=1, replica_groups=mesh['x'=4,'h'=2,'l'=2,'z'=4,'c'=2] {'l','z'}, dimensions={0} | all-to-all | bytes 2097152 | tf_op jit(solution)/shard_map/all_to_all | solution.py:237
  43.5 2.2 %shard_map.62 = f32[16,1,4,16,256]{4,3,2,1,0:T(8,128)} custom-call(s32[4,16]{1,0:T(4,128)S(1)} %copy-done.2, f32[1,2,4,256,256]{4,3,2,1,0:T(8,128)S(1)} %copy-done.1, f32[1,2,4,256,256]{4,3,2,1,0:T(8,128)S(1)} %collective-permute-done.theirs, f32[8,4,32,256]{3,2,1,0:T(8,128)S(1)} %all_to_all.41.refs_0_), custom_call_target="tpu_custom_call" | custom-call | flops 1000000000 | bytes 2097152 | tf_op jit(solution)/shard_map/pallas_call | solution.py:220
  45.7 5.4 %all-to-all-start.2 = ((f32[16,1,4,16,256]{4,3,2,1,0:T(8,128)}), f32[16,1,4,16,256]{4,3,2,1,0:T(8,128)}, u32[]{:S(2)}, u32[]{:S(2)}) async-start(f32[16,1,4,16,256]{4,3,2,1,0:T(8,128)} %shard_map.62), calls=%async_computation.2 | async-start | bytes 2097152 | tf_op jit(solution)/shard_map/all_to_all | solution.py:237
  51.2 3.2 %collective-permute-start.2 = (f32[8,4,32,256]{3,2,1,0:T(8,128)S(1)}, f32[8,4,32,256]{3,2,1,0:T(8,128)S(1)}, u32[]{:S(2)}, u32[]{:S(2)}) collective-permute-start(f32[8,4,32,256]{3,2,1,0:T(8,128)S(1)} %all_to_all.41.refs_0_), channel_id=1, source_target_pairs={{0,32},{32,64},{64,96},{96,0},{1,33},{33,65},{65,97},{97,1},{2,34}... | collective-permute-start | bytes 3145736 | tf_op jit(solution)/shard_map/ppermute | solution.py:233
  54.4 0.9 collective-permute-start.3
  55.3 11.0 %all-to-all-done.2 = f32[16,1,4,16,256]{4,3,2,1,0:T(8,128)} async-done(((f32[16,1,4,16,256]{4,3,2,1,0:T(8,128)}), f32[16,1,4,16,256]{4,3,2,1,0:T(8,128)}, u32[]{:S(2)}, u32[]{:S(2)}) %all-to-all-start.2) | async-done | bytes 1048608 | tf_op jit(solution)/shard_map/all_to_all | solution.py:237
  66.2 1.3 bitcast_reduce_fusion.1.refs_2_.refs_0_
  67.6 8.7 %collective-permute-done.2.refs_0_ = f32[8,4,32,256]{3,2,1,0:T(8,128)S(1)} collective-permute-done((f32[8,4,32,256]{3,2,1,0:T(8,128)S(1)}, f32[8,4,32,256]{3,2,1,0:T(8,128)S(1)}, u32[]{:S(2)}, u32[]{:S(2)}) %collective-permute-start.2) | collective-permute-done | bytes 1048608 | tf_op jit(solution)/shard_map/ppermute | solution.py:233
  76.3 1.2 collective-permute-done.3.refs_1_
  77.4 8.9 %shard_map.63.refs_2_ = f32[16,2,4,16,256]{4,3,2,1,0:T(8,128)} custom-call(s32[4,16]{1,0:T(4,128)S(1)} %copy-done.2, f32[3,2,4,256,256]{4,3,2,1,0:T(8,128)} %get-tuple-element.12.mine, f32[3,2,4,256,256]{4,3,2,1,0:T(8,128)} %collective-permute-done.1.theirs, f32[8,4,32,256]{3,2,1,0:T(8,128)S(1)} %collective-permute-done.2.refs_0_, ...), custom_call_target="tpu_custom_call" | custom-call | flops 2000000000 | bytes 4194304 | tf_op jit(solution)/shard_map/pallas_call | solution.py:220
  86.4 4.5 %all-to-all-start.3 = ((f32[16,2,4,16,256]{4,3,2,1,0:T(8,128)}), f32[16,2,4,16,256]{4,3,2,1,0:T(8,128)}, u32[]{:S(2)}, u32[]{:S(2)}) async-start(f32[16,2,4,16,256]{4,3,2,1,0:T(8,128)} %shard_map.63.refs_2_), calls=%async_computation.3 | async-start | bytes 4194304 | tf_op jit(solution)/shard_map/all_to_all | solution.py:237
  90.9 1.1 collective-permute-start.4
  92.0 1.8 collective-permute-start.5
  93.8 9.5 %collective-permute-done.4.refs_0_ = f32[4,4,32,256]{3,2,1,0:T(8,128)S(1)} collective-permute-done((f32[4,4,32,256]{3,2,1,0:T(8,128)S(1)}, f32[4,4,32,256]{3,2,1,0:T(8,128)S(1)}, u32[]{:S(2)}, u32[]{:S(2)}) %collective-permute-start.4) | collective-permute-done | bytes 524320 | tf_op jit(solution)/shard_map/ppermute | solution.py:233
  103.3 3.9 %shard_map.64 = f32[16,1,4,16,256]{4,3,2,1,0:T(8,128)} custom-call(s32[4,16]{1,0:T(4,128)S(1)} %copy-done.2, f32[3,2,4,256,256]{4,3,2,1,0:T(8,128)} %get-tuple-element.12.mine, f32[3,2,4,256,256]{4,3,2,1,0:T(8,128)} %collective-permute-done.1.theirs, f32[4,4,32,256]{3,2,1,0:T(8,128)S(1)} %collective-permute-done.4.refs_0_, ...), custom_call_target="tpu_custom_call" | custom-call | flops 1000000000 | bytes 2097152 | tf_op jit(solution)/shard_map/pallas_call | solution.py:220
  107.1 9.4 %all-to-all-done.3 = f32[16,2,4,16,256]{4,3,2,1,0:T(8,128)} async-done(((f32[16,2,4,16,256]{4,3,2,1,0:T(8,128)}), f32[16,2,4,16,256]{4,3,2,1,0:T(8,128)}, u32[]{:S(2)}, u32[]{:S(2)}) %all-to-all-start.3) | async-done | bytes 2097184 | tf_op jit(solution)/shard_map/all_to_all | solution.py:237
  116.6 1.8 slice_reduce_fusion
  118.3 5.7 %all-to-all-start.4 = ((f32[16,1,4,16,256]{4,3,2,1,0:T(8,128)}), f32[16,1,4,16,256]{4,3,2,1,0:T(8,128)}, u32[]{:S(2)}, u32[]{:S(2)}) async-start(f32[16,1,4,16,256]{4,3,2,1,0:T(8,128)} %shard_map.64), calls=%async_computation.4 | async-start | bytes 2097152 | tf_op jit(solution)/shard_map/all_to_all | solution.py:237
  124.0 0.6 collective-permute-start.6
  124.6 1.2 collective-permute-start.8
  125.8 10.3 %all-to-all-done.4 = f32[16,1,4,16,256]{4,3,2,1,0:T(8,128)} async-done(((f32[16,1,4,16,256]{4,3,2,1,0:T(8,128)}), f32[16,1,4,16,256]{4,3,2,1,0:T(8,128)}, u32[]{:S(2)}, u32[]{:S(2)}) %all-to-all-start.4) | async-done | bytes 1048608 | tf_op jit(solution)/shard_map/all_to_all | solution.py:237
  136.1 1.3 bitcast_reduce_fusion
  137.5 5.3 %collective-permute-done.7.refs_2_ = f32[2,4,16,256]{3,2,1,0:T(8,128)S(1)} collective-permute-done((f32[2,4,16,256]{3,2,1,0:T(8,128)S(1)}, f32[2,4,16,256]{3,2,1,0:T(8,128)S(1)}, u32[]{:S(2)}, u32[]{:S(2)}) %collective-permute-start.7) | collective-permute-done | bytes 131104 | tf_op jit(solution)/shard_map/ppermute | solution.py:233
  142.8 1.0 shard_map.65
  143.7 22.3 %all_to_all.42 = f32[32,16,256]{2,1,0:T(8,128)S(1)} all-to-all(f32[32,16,256]{2,1,0:T(8,128)S(1)} %shard_map.65), channel_id=1, replica_groups=mesh['x'=4,'h'=2,'l'=2,'z'=4,'c'=2] {'h','l','z','c'}, dimensions={0} | all-to-all | bytes 1048576 | tf_op jit(solution)/shard_map/all_to_all | solution.py:237
  166.0 1.5 shard_map.66
  167.6 1.7 collective-permute-start.9
  169.3 1.1 collective-permute-start.10
  170.3 0.7 add.32
  171.1 3.9 %all-to-all-start.6 = ((f32[32,8,256]{2,1,0:T(8,128)}), f32[32,8,256]{2,1,0:T(8,128)S(1)}, u32[]{:S(2)}, u32[]{:S(2)}) async-start(f32[32,8,256]{2,1,0:T(8,128)} %bitcast.10), calls=%async_computation.6 | async-start | bytes 524288 | tf_op jit(solution)/shard_map/all_to_all | solution.py:237
  175.0 10.5 %all-to-all-done.6 = f32[32,8,256]{2,1,0:T(8,128)S(1)} async-done(((f32[32,8,256]{2,1,0:T(8,128)}), f32[32,8,256]{2,1,0:T(8,128)S(1)}, u32[]{:S(2)}, u32[]{:S(2)}) %all-to-all-start.6) | async-done | bytes 262176 | tf_op jit(solution)/shard_map/all_to_all | solution.py:237
  185.5 0.7 broadcast_in_dim.22
  186.2 3.4 %all-to-all-start.7 = ((f32[8,4,8,256]{3,2,1,0:T(8,128)}), f32[8,4,8,256]{3,2,1,0:T(8,128)S(1)}, u32[]{:S(2)}, u32[]{:S(2)}) async-start(f32[8,4,8,256]{3,2,1,0:T(8,128)} %broadcast_in_dim.22), calls=%async_computation.7 | async-start | bytes 524288 | tf_op jit(solution)/shard_map/all_to_all | solution.py:237
  189.7 0.2 collective-permute-start.11
  189.9 2.6 %collective-permute-start.12 = (f32[128,512]{1,0:T(8,128)S(1)}, f32[128,512]{1,0:T(8,128)S(1)}, u32[]{:S(2)}, u32[]{:S(2)}) collective-permute-start(f32[128,512]{1,0:T(8,128)S(1)} %slice.29), channel_id=1, source_target_pairs={{0,96},{32,0},{64,32},{96,64},{1,97},{33,1},{65,33},{97,65},{2,98}... | collective-permute-start | bytes 786440 | tf_op jit(solution)/shard_map/ppermute | solution.py:233
  192.5 0.8 bitcast_dynamic-update-slice_fusion.1
  193.4 0.8 bitcast_dynamic-update-slice_fusion
  194.2 1.5 all-to-all-done.7
  195.7 3.3 %collective-permute-start.14 = (f32[4,64,256]{2,1,0:T(8,128)S(1)}, f32[4,64,256]{2,1,0:T(8,128)S(1)}, u32[]{:S(2)}, u32[]{:S(2)}) collective-permute-start(f32[4,64,256]{2,1,0:T(8,128)S(1)} %bitcast.29), channel_id=1, source_target_pairs={{0,1},{1,0},{2,3},{3,2},{4,5},{5,4},{6,7},{7,6},{8,9},{9,8},{10,11... | collective-permute-start | bytes 786440 | tf_op jit(solution)/shard_map/ppermute | solution.py:233
  199.1 0.7 bitcast_dynamic-update-slice_fusion.3
  199.8 0.7 bitcast_dynamic-update-slice_fusion.2
  200.5 0.9 fusion
  (29 shorter events, 0.4 us)
Async XLA Ops:
  3.2 5.9 %copy-start.3 = (f32[8,2,32,256]{3,2,1,0:T(8,128)S(1)}, f32[8,2,32,256]{3,2,1,0:T(8,128)}, u32[]{:S(2)}) copy-start(f32[8,2,32,256]{3,2,1,0:T(8,128)} %shard_map.59.after) | copy-start | bytes 1572868
  3.2 22.0 %copy-start.2 = (s32[4,16]{1,0:T(4,128)S(1)}, s32[4,16]{1,0:T(4,128)}, u32[]{:S(2)}) copy-start(s32[4,16]{1,0:T(4,128)} %fs.15) | copy-start | bytes 772
  7.8 69.6 %collective-permute-start.1 = (f32[3,2,4,256,256]{4,3,2,1,0:T(8,128)}, f32[3,2,4,256,256]{4,3,2,1,0:T(8,128)}, u32[]{:S(2)}, u32[]{:S(2)}) collective-permute-start(f32[3,2,4,256,256]{4,3,2,1,0:T(8,128)} %get-tuple-element.12.mine), channel_id=1, source_target_pairs={{0,1},{1,0},{2,3},{3,2},{4,5},{5,4},{6,7},{7,6},{8,9},{9,8},{10,11... | collective-permute-start | bytes 18874376 | tf_op jit(solution)/shard_map/ppermute | solution.py:233
  9.0 34.5 %collective-permute-start = (f32[1,2,4,256,256]{4,3,2,1,0:T(8,128)}, f32[1,2,4,256,256]{4,3,2,1,0:T(8,128)S(1)}, u32[]{:S(2)}, u32[]{:S(2)}) collective-permute-start(f32[1,2,4,256,256]{4,3,2,1,0:T(8,128)} %get-tuple-element.11.mine), channel_id=1, source_target_pairs={{0,1},{1,0},{2,3},{3,2},{4,5},{5,4},{6,7},{7,6},{8,9},{9,8},{10,11... | collective-permute-start | bytes 6291464 | tf_op jit(solution)/shard_map/ppermute | solution.py:233
  25.2 18.2 %copy-start.1 = (f32[1,2,4,256,256]{4,3,2,1,0:T(8,128)S(1)}, f32[1,2,4,256,256]{4,3,2,1,0:T(8,128)}, u32[]{:S(2)}) copy-start(f32[1,2,4,256,256]{4,3,2,1,0:T(8,128)} %get-tuple-element.11.mine) | copy-start | bytes 6291460
  45.7 20.5 %all-to-all-start.2 = ((f32[16,1,4,16,256]{4,3,2,1,0:T(8,128)}), f32[16,1,4,16,256]{4,3,2,1,0:T(8,128)}, u32[]{:S(2)}, u32[]{:S(2)}) async-start(f32[16,1,4,16,256]{4,3,2,1,0:T(8,128)} %shard_map.62), calls=%async_computation.2 | async-start | bytes 2097152 | tf_op jit(solution)/shard_map/all_to_all | solution.py:237
  51.2 25.1 %collective-permute-start.2 = (f32[8,4,32,256]{3,2,1,0:T(8,128)S(1)}, f32[8,4,32,256]{3,2,1,0:T(8,128)S(1)}, u32[]{:S(2)}, u32[]{:S(2)}) collective-permute-start(f32[8,4,32,256]{3,2,1,0:T(8,128)S(1)} %all_to_all.41.refs_0_), channel_id=1, source_target_pairs={{0,32},{32,64},{64,96},{96,0},{1,33},{33,65},{65,97},{97,1},{2,34}... | collective-permute-start | bytes 3145736 | tf_op jit(solution)/shard_map/ppermute | solution.py:233
  54.4 23.1 %collective-permute-start.3 = (f32[8,4,32,256]{3,2,1,0:T(8,128)S(1)}, f32[8,4,32,256]{3,2,1,0:T(8,128)S(1)}, u32[]{:S(2)}, u32[]{:S(2)}) collective-permute-start(f32[8,4,32,256]{3,2,1,0:T(8,128)S(1)} %all_to_all.41.refs_0_), channel_id=1, source_target_pairs={{0,96},{32,0},{64,32},{96,64},{1,97},{33,1},{65,33},{97,65},{2,98}... | collective-permute-start | bytes 3145736 | tf_op jit(solution)/shard_map/ppermute | solution.py:233
  86.4 30.2 %all-to-all-start.3 = ((f32[16,2,4,16,256]{4,3,2,1,0:T(8,128)}), f32[16,2,4,16,256]{4,3,2,1,0:T(8,128)}, u32[]{:S(2)}, u32[]{:S(2)}) async-start(f32[16,2,4,16,256]{4,3,2,1,0:T(8,128)} %shard_map.63.refs_2_), calls=%async_computation.3 | async-start | bytes 4194304 | tf_op jit(solution)/shard_map/all_to_all | solution.py:237
  90.9 12.3 %collective-permute-start.4 = (f32[4,4,32,256]{3,2,1,0:T(8,128)S(1)}, f32[4,4,32,256]{3,2,1,0:T(8,128)S(1)}, u32[]{:S(2)}, u32[]{:S(2)}) collective-permute-start(f32[4,4,32,256]{3,2,1,0:T(8,128)S(1)} %slice.26), channel_id=1, source_target_pairs={{0,32},{32,64},{64,96},{96,0},{1,33},{33,65},{65,97},{97,1},{2,34}... | collective-permute-start | bytes 1572872 | tf_op jit(solution)/shard_map/ppermute | solution.py:233
  92.0 11.3 %collective-permute-start.5 = (f32[4,4,32,256]{3,2,1,0:T(8,128)S(1)}, f32[4,4,32,256]{3,2,1,0:T(8,128)S(1)}, u32[]{:S(2)}, u32[]{:S(2)}) collective-permute-start(f32[4,4,32,256]{3,2,1,0:T(8,128)S(1)} %slice.27), channel_id=1, source_target_pairs={{0,96},{32,0},{64,32},{96,64},{1,97},{33,1},{65,33},{97,65},{2,98}... | collective-permute-start | bytes 1572872 | tf_op jit(solution)/shard_map/ppermute | solution.py:233
  118.3 17.7 %all-to-all-start.4 = ((f32[16,1,4,16,256]{4,3,2,1,0:T(8,128)}), f32[16,1,4,16,256]{4,3,2,1,0:T(8,128)}, u32[]{:S(2)}, u32[]{:S(2)}) async-start(f32[16,1,4,16,256]{4,3,2,1,0:T(8,128)} %shard_map.64), calls=%async_computation.4 | async-start | bytes 2097152 | tf_op jit(solution)/shard_map/all_to_all | solution.py:237
  124.0 42.0 %copy-start = (f32[4,1,256,512]{3,2,1,0:T(8,128)S(1)}, f32[4,1,256,512]{3,2,1,0:T(8,128)}, u32[]{:S(2)}) copy-start(f32[4,1,256,512]{3,2,1,0:T(8,128)} %panels.3) | copy-start | bytes 6291460
  124.0 13.4 %collective-permute-start.6 = (f32[2,4,16,256]{3,2,1,0:T(8,128)S(1)}, f32[2,4,16,256]{3,2,1,0:T(8,128)S(1)}, u32[]{:S(2)}, u32[]{:S(2)}) collective-permute-start(f32[2,4,16,256]{3,2,1,0:T(8,128)S(1)} %get-tuple-element.13), channel_id=1, source_target_pairs={{0,96},{32,0},{64,32},{96,64},{1,97},{33,1},{65,33},{97,65},{2,98}... | collective-permute-start | bytes 393224 | tf_op jit(solution)/shard_map/ppermute | solution.py:233
  124.6 12.9 %collective-permute-start.8 = (f32[2,4,16,256]{3,2,1,0:T(8,128)S(1)}, f32[2,4,16,256]{3,2,1,0:T(8,128)S(1)}, u32[]{:S(2)}, u32[]{:S(2)}) collective-permute-start(f32[2,4,16,256]{3,2,1,0:T(8,128)S(1)} %get-tuple-element.15), channel_id=1, source_target_pairs={{0,32},{32,64},{64,96},{96,0},{1,33},{33,65},{65,97},{97,1},{2,34}... | collective-permute-start | bytes 393224 | tf_op jit(solution)/shard_map/ppermute | solution.py:233
  137.4 5.4 %collective-permute-start.7 = (f32[2,4,16,256]{3,2,1,0:T(8,128)S(1)}, f32[2,4,16,256]{3,2,1,0:T(8,128)S(1)}, u32[]{:S(2)}, u32[]{:S(2)}) collective-permute-start(f32[2,4,16,256]{3,2,1,0:T(8,128)S(1)} %bitcast_reduce_fusion), channel_id=1, source_target_pairs={{0,64},{32,96},{64,0},{96,32},{1,65},{33,97},{65,1},{97,33},{2,66}... | collective-permute-start | bytes 393224 | tf_op jit(solution)/shard_map/ppermute | solution.py:233
  167.5 2.8 %collective-permute-start.13 = (f32[4,8,8,256]{3,2,1,0:T(8,128)S(1)}, f32[4,8,8,256]{3,2,1,0:T(8,128)S(1)}, u32[]{:S(2)}, u32[]{:S(2)}) collective-permute-start(f32[4,8,8,256]{3,2,1,0:T(8,128)S(1)} %get-tuple-element.19), channel_id=1, source_target_pairs={{0,1},{1,0},{2,3},{3,2},{4,5},{5,4},{6,7},{7,6},{8,9},{9,8},{10,11... | collective-permute-start | bytes 786440 | tf_op jit(solution)/shard_map/ppermute | solution.py:233
  167.6 22.1 %collective-permute-start.9 = (f32[256,512]{1,0:T(8,128)S(1)}, f32[256,512]{1,0:T(8,128)S(1)}, u32[]{:S(2)}, u32[]{:S(2)}) collective-permute-start(f32[256,512]{1,0:T(8,128)S(1)} %get-tuple-element.17), channel_id=1, source_target_pairs={{0,32},{32,64},{64,96},{96,0},{1,33},{33,65},{65,97},{97,1},{2,34}... | collective-permute-start | bytes 1572872 | tf_op jit(solution)/shard_map/ppermute | solution.py:233
  169.3 20.7 %collective-permute-start.10 = (f32[256,512]{1,0:T(8,128)S(1)}, f32[256,512]{1,0:T(8,128)S(1)}, u32[]{:S(2)}, u32[]{:S(2)}) collective-permute-start(f32[256,512]{1,0:T(8,128)S(1)} %get-tuple-element.17), channel_id=1, source_target_pairs={{0,96},{32,0},{64,32},{96,64},{1,97},{33,1},{65,33},{97,65},{2,98}... | collective-permute-start | bytes 1572872 | tf_op jit(solution)/shard_map/ppermute | solution.py:233
  171.1 14.4 %all-to-all-start.6 = ((f32[32,8,256]{2,1,0:T(8,128)}), f32[32,8,256]{2,1,0:T(8,128)S(1)}, u32[]{:S(2)}, u32[]{:S(2)}) async-start(f32[32,8,256]{2,1,0:T(8,128)} %bitcast.10), calls=%async_computation.6 | async-start | bytes 524288 | tf_op jit(solution)/shard_map/all_to_all | solution.py:237
  186.2 9.5 %all-to-all-start.7 = ((f32[8,4,8,256]{3,2,1,0:T(8,128)}), f32[8,4,8,256]{3,2,1,0:T(8,128)S(1)}, u32[]{:S(2)}, u32[]{:S(2)}) async-start(f32[8,4,8,256]{3,2,1,0:T(8,128)} %broadcast_in_dim.22), calls=%async_computation.7 | async-start | bytes 524288 | tf_op jit(solution)/shard_map/all_to_all | solution.py:237
  189.7 10.8 %copy-start.4 = (f32[4,64,512]{2,1,0:T(8,128)S(1)}, f32[4,64,512]{2,1,0:T(8,128)}, u32[]{:S(2)}) copy-start(f32[4,64,512]{2,1,0:T(8,128)} %param.6) | copy-start | bytes 1572868
  189.7 9.4 %collective-permute-start.11 = (f32[128,512]{1,0:T(8,128)S(1)}, f32[128,512]{1,0:T(8,128)S(1)}, u32[]{:S(2)}, u32[]{:S(2)}) collective-permute-start(f32[128,512]{1,0:T(8,128)S(1)} %slice.28), channel_id=1, source_target_pairs={{0,32},{32,64},{64,96},{96,0},{1,33},{33,65},{65,97},{97,1},{2,34}... | collective-permute-start | bytes 786440 | tf_op jit(solution)/shard_map/ppermute | solution.py:233
  189.9 9.8 %collective-permute-start.12 = (f32[128,512]{1,0:T(8,128)S(1)}, f32[128,512]{1,0:T(8,128)S(1)}, u32[]{:S(2)}, u32[]{:S(2)}) collective-permute-start(f32[128,512]{1,0:T(8,128)S(1)} %slice.29), channel_id=1, source_target_pairs={{0,96},{32,0},{64,32},{96,64},{1,97},{33,1},{65,33},{97,65},{2,98}... | collective-permute-start | bytes 786440 | tf_op jit(solution)/shard_map/ppermute | solution.py:233
  195.7 4.8 %collective-permute-start.14 = (f32[4,64,256]{2,1,0:T(8,128)S(1)}, f32[4,64,256]{2,1,0:T(8,128)S(1)}, u32[]{:S(2)}, u32[]{:S(2)}) collective-permute-start(f32[4,64,256]{2,1,0:T(8,128)S(1)} %bitcast.29), channel_id=1, source_target_pairs={{0,1},{1,0},{2,3},{3,2},{4,5},{5,4},{6,7},{7,6},{8,9},{9,8},{10,11... | collective-permute-start | bytes 786440 | tf_op jit(solution)/shard_map/ppermute | solution.py:233
